TPU v7x, 512 devices: a whole 4x8x8 slice. The times are simulated.
512 devices in a mesh: gx: 32 (over x, z), gy: 16 (over y, core).
Axes of the slice: x: 4, y: 8, z: 8, core: 2. Of those that a mesh axis runs over, the one named last changes fastest.
Arguments:
- seeds: int32 [64, 1024], P('gy', 'gx'), may hold values from 0 to 1073741823
- lengths: float32 [3], replicated, may hold values from 3 to 24
- exponents: float32 [3], replicated, may hold values from 1.5 to 2.5
- storage: float32 [64, 1024, 1024], P('gy', 'gx'), may hold values from 0.5 to 8
- recharge: float32 [64, 1024, 1024], P('gy', 'gx'), may hold values from -36 to 36
- well_cells: int32 [3, 256], replicated, may hold values from 0 to 1023, as said below
- well_rates: float32 [256], replicated, may hold values from -180 to 180
Outputs:
- log_perm: float32 [64, 1024, 1024], P('gy', 'gx')
- pressure: float32 [64, 1024, 1024], P('gy', 'gx')
- residual: float32 [64, 1024, 1024], P('gy', 'gx')
Inputs may be any that keep to these rules, and one draw needn't show every extreme that they name: Row 0 of well_cells gives each well's layer, below 64; rows 1 and 2 its cell along the second and third dimensions, below 1024 and 1024. Wells may share a cell; their rates then add.
All inputs are finite; a program needn't handle non-finite values.
Results may differ from a plain program's by a relative error of at most 0.00024.
Values sent between devices are 32-bit elements; how exact they have to be, the bound alone decides.
No kernel may reach another device: no remote copies, remote signals or barrier semaphores. Data moves between devices by JAX's collectives and lax.ppermute only.
A program may use at most 128 MiB of HBM per device.

v0:
```python
import math

import jax
import jax.numpy as jnp
from jax import lax
from jax.sharding import PartitionSpec as P

LZ = 64
LX = 1024
LY = 1024
ITERS = 3


AMPLITUDE = 4.0
HIGHEST = lax.Precision.HIGHEST


def padded_2(block, sides, width):
    for axis, dim in sides:
        count = lax.axis_size(axis)
        forward = [(i, i + 1) for i in range(count - 1)]
        backward = [(target, source) for source, target in forward]
        low = lax.ppermute(
            lax.slice_in_dim(block, block.shape[dim] - width, None, axis=dim), axis, forward
        )
        high = lax.ppermute(lax.slice_in_dim(block, 0, width, axis=dim), axis, backward)
        block = jnp.concatenate([low, block, high], axis=dim)
    return block


def mix_bits(seed_rows, cells):
    hashed = seed_rows + cells * jnp.int32(-1640531535)
    hashed = hashed ^ hashed >> 16 & 65535
    hashed = hashed * jnp.int32(-2048144789)
    hashed = hashed ^ hashed >> 13 & 524287
    hashed = hashed * jnp.int32(-1028477387)
    hashed = hashed ^ hashed >> 16 & 65535
    value = (hashed >> 8 & 16777215).astype(jnp.float32)
    return (value + 0.5) * (2.0 * math.sqrt(3.0) / 16777216.0) - math.sqrt(3.0)


def magnitude(index, length):
    folded = jnp.minimum(index, length - index)
    return folded.astype(jnp.float32) * (2.0 * math.pi / length)


def filter_gain(wave_z, wave_x, wave_y, lengths, exponents):
    total = 1.0 + jnp.power(lengths[0] * wave_z, exponents[0])
    total = total + jnp.power(lengths[1] * wave_x, exponents[1])
    total = total + jnp.power(lengths[2] * wave_y, exponents[2])
    return AMPLITUDE * jnp.sqrt(lengths[0] * lengths[1] * lengths[2]) / total


def dft_tables(length):
    index = jnp.arange(length, dtype=jnp.int32)
    phase = index[:, None] * index[None, :] % length
    angle = phase.astype(jnp.float32) * (2.0 * math.pi / length)
    return (jnp.cos(angle), jnp.sin(angle))


def contract(form, data, table):
    return jnp.einsum(form, data, table, precision=HIGHEST, preferred_element_type=jnp.float32)


def transform(form, pair, tables, sign):
    real_cos = contract(form, pair[0], tables[0])
    real_sin = contract(form, pair[0], tables[1])
    imag_cos = contract(form, pair[1], tables[0])
    imag_sin = contract(form, pair[1], tables[1])
    return (real_cos + sign * imag_sin, imag_cos - sign * real_sin)


def harmonic(centre, other):
    return 2.0 * centre * other / (centre + other)


def neighbours(padded):
    centre = padded[1:-1, 1:-1, :]
    y_low = jnp.pad(centre[:, :, :-1], ((0, 0), (0, 0), (1, 0)))
    y_high = jnp.pad(centre[:, :, 1:], ((0, 0), (0, 0), (0, 1)))
    return [
        padded[:-2, 1:-1, :],
        padded[2:, 1:-1, :],
        padded[1:-1, :-2, :],
        padded[1:-1, 2:, :],
        y_low,
        y_high,
    ]


def shards(seeds, lengths, exponents, storage, recharge, well_cells, well_rates):
    layers = storage.shape[0]
    rows_here = storage.shape[1]
    cells = jnp.arange(LY, dtype=jnp.int32)
    noise = mix_bits(seeds[:, :, None], cells[None, None, :])
    tables_y = dft_tables(LY)
    tables_z = dft_tables(LZ)
    scale = 1.0 / (LZ * LX * LY)
    columns = LY // 2
    column_index = jnp.arange(columns, dtype=jnp.int32)
    weights = jnp.where(column_index == 0, 1.0, 2.0).astype(jnp.float32)
    forward_cos = tables_y[0][:, :columns]
    forward_sin = tables_y[1][:, :columns]
    back_cos = tables_y[0][:columns, :] * weights[:, None]
    back_sin = tables_y[1][:columns, :] * weights[:, None]
    spec_real = contract("zxy,yk->zxk", noise, forward_cos)
    spec_imag = -contract("zxy,yk->zxk", noise, forward_sin)

    def across_gx(pair):
        return (
            lax.all_to_all(pair[0], "gx", split_axis=2, concat_axis=1, tiled=True),
            lax.all_to_all(pair[1], "gx", split_axis=2, concat_axis=1, tiled=True),
        )

    def across_gy(pair):
        return (
            lax.all_to_all(pair[0], "gy", split_axis=2, concat_axis=0, tiled=True),
            lax.all_to_all(pair[1], "gy", split_axis=2, concat_axis=0, tiled=True),
        )

    pair = transform("zxk,xm->zkm", across_gx((spec_real, spec_imag)), tables_y, 1.0)
    pair = transform("zkm,zn->nkm", across_gy(pair), tables_z, 1.0)
    block_y = pair[0].shape[1]
    block_x = pair[0].shape[2]
    wave_z = magnitude(jnp.arange(LZ, dtype=jnp.int32), LZ)
    y_index = jnp.arange(block_y, dtype=jnp.int32) + lax.axis_index("gx") * block_y
    wave_y = magnitude(y_index, LY)
    keep_y = (y_index != LY // 2).astype(jnp.float32)
    wave_x = magnitude(jnp.arange(block_x, dtype=jnp.int32) + lax.axis_index("gy") * block_x, LX)
    gain = filter_gain(
        wave_z[:, None, None], wave_x[None, None, :], wave_y[None, :, None], lengths, exponents
    )
    gain = gain * (keep_y * scale)[None, :, None]
    pair = transform("nkm,nz->mkz", (pair[0] * gain, pair[1] * gain), tables_z, -1.0)
    pair = transform("xkz,xm->zkm", across_gy(pair), tables_y, -1.0)
    pair = across_gx(pair)
    log_perm = contract("zkx,ky->zxy", pair[0], back_cos) - contract(
        "zkx,ky->zxy", pair[1], back_sin
    )
    perm = jnp.exp(log_perm)
    perm_near = padded_2(perm, (("gx", 1), ("gy", 0)), 1)
    conduct = [harmonic(perm, other) for other in neighbours(perm_near)]
    diag = storage
    for face in conduct:
        diag = diag + face
    local_layer = well_cells[0] - lax.axis_index("gy") * layers
    local_row = well_cells[1] - lax.axis_index("gx") * rows_here
    inside = (
        (local_layer >= 0) & (local_layer < layers) & (local_row >= 0) & (local_row < rows_here)
    )
    local_layer = jnp.where(inside, local_layer, layers)
    local_row = jnp.where(inside, local_row, rows_here)
    rhs = recharge.at[local_layer, local_row, well_cells[2]].add(well_rates, mode="drop")
    pressure = jnp.zeros_like(rhs)
    residual = rhs

    def global_dot(first, second):
        return lax.psum(jnp.sum(first * second), ("gx", "gy"))

    precond = residual / diag
    direction = precond
    rz_now = global_dot(residual, precond)
    for step in range(ITERS):
        padded = padded_2(direction, (("gx", 1), ("gy", 0)), 1)
        result = storage * direction
        for apply_face, apply_other in zip(conduct, neighbours(padded)):
            result = result + apply_face * (direction - apply_other)
        alpha = rz_now / global_dot(direction, result)
        pressure = pressure + alpha * direction
        residual = residual - alpha * result
        precond = residual / diag
        rz_next = global_dot(residual, precond)
        direction = precond + rz_next / rz_now * direction
        rz_now = rz_next
    return (log_perm, pressure, residual)


def solution(mesh):
    placed = (P("gy", "gx"), P(), P(), P("gy", "gx", None), P("gy", "gx", None), P(), P())
    return jax.shard_map(
        shards,
        mesh=mesh,
        in_specs=placed,
        out_specs=(P("gy", "gx", None), P("gy", "gx", None), P("gy", "gx", None)),
        check_vma=False,
    )
```

profile of v0, /device:TPU:1, one launch (start us, length us, event | category | flops | bytes accessed | tf_op | source)
XLA Modules:
  0.0 942.4 jit_solution(10838407166717327817)
XLA Ops:
  0.6 15.6 %fusion.30 = f32[1024,1024]{1,0:T(8,128)S(1)} fusion(), kind=kLoop, calls=%fused_computation.36 | loop fusion | flops 14680064 | bytes 4194304 | tf_op jit(solution)/shard_map/sin | solution.py:58
  21.5 13.7 %all-to-all-start.1 = ((f32[32,1,2048]{2,1,0:T(1,128)}), f32[32,1,2048]{2,1,0:T(1,128)S(1)}, u32[]{:S(2)}, u32[]{:S(2)}) async-start(f32[32,1,2048]{2,1,0:T(1,128)} %reshape.216), calls=%async_computation.1 | async-start | bytes 524288 | tf_op jit(solution)/shard_map/all_to_all | solution.py:112
  35.2 15.3 %fusion.31 = f32[1024,1024]{1,0:T(8,128)S(1)} fusion(), kind=kLoop, calls=%fused_computation.37 | loop fusion | flops 14680064 | bytes 4194304 | tf_op jit(solution)/shard_map/cos | solution.py:58
  59.6 9.4 %all-to-all-start = ((f32[32,1,2048]{2,1,0:T(1,128)}), f32[32,1,2048]{2,1,0:T(1,128)S(1)}, u32[]{:S(2)}, u32[]{:S(2)}) async-start(f32[32,1,2048]{2,1,0:T(1,128)} %reshape.218), calls=%async_computation | async-start | bytes 524288 | tf_op jit(solution)/shard_map/all_to_all | solution.py:111
  72.3 18.2 %fusion.9 = f32[4,16,1024]{2,1,0:T(8,128)S(1)} fusion(f32[4,1024,16]{1,2,0:T(8,128)S(1)} %all_to_all.111), kind=kOutput, calls=%fused_computation.13 | convolution fusion | flops 819986432 | bytes 524288 | tf_op jit(solution)/shard_map/zxk,xm->zkm/dot_general | solution.py:62
  93.3 18.5 %fusion.7 = f32[4,16,1024]{2,1,0:T(8,128)S(1)} fusion(f32[4,1024,16]{1,2,0:T(8,128)S(1)} %all_to_all.107), kind=kOutput, calls=%fused_computation.11 | convolution fusion | flops 819986432 | bytes 524288 | tf_op jit(solution)/shard_map/zxk,xm->zkm/dot_general | solution.py:62
  111.8 18.1 %fusion.50 = f32[4,16,1024]{2,1,0:T(8,128)S(1)} fusion(f32[4,16,1024]{2,1,0:T(8,128)S(1)} %fusion.9, f32[4,1024,16]{1,2,0:T(8,128)S(1)} %all_to_all.107), kind=kOutput, calls=%fused_computation.50 | convolution fusion | flops 820051968 | bytes 786432 | tf_op jit(solution)/shard_map/zxk,xm->zkm/dot_general | solution.py:62
  133.0 9.2 all-to-all-start.2
  142.2 18.1 %fusion.53 = f32[4,16,1024]{2,1,0:T(8,128)S(1)} fusion(f32[4,16,1024]{2,1,0:T(8,128)S(1)} %fusion.7, f32[4,1024,16]{1,2,0:T(8,128)S(1)} %all_to_all.111), kind=kOutput, calls=%fused_computation.51 | convolution fusion | flops 820051968 | bytes 786432 | tf_op jit(solution)/shard_map/zxk,xm->zkm/dot_general | solution.py:62
  163.4 7.5 all-to-all-start.3
  199.4 8.8 all-to-all-done.4
  213.8 18.5 %fusion.71 = f32[1024,16,4]{0,1,2:T(8,128)S(1)} fusion(f32[1024,16,4]{0,1,2:T(8,128)S(1)} %all_to_all.123), kind=kOutput, calls=%fused_computation.57 | convolution fusion | flops 820051968 | bytes 524288 | tf_op jit(solution)/shard_map/xkz,xm->zkm/dot_general | solution.py:62
  234.3 18.9 %fusion.68 = f32[1024,16,4]{0,1,2:T(8,128)S(1)} fusion(f32[1024,16,4]{0,1,2:T(8,128)S(1)} %all_to_all.127), kind=kOutput, calls=%fused_computation.56 | convolution fusion | flops 820051968 | bytes 524288 | tf_op jit(solution)/shard_map/xkz,xm->zkm/dot_general | solution.py:62
  253.3 18.4 %fusion.65 = f32[4,16,1024]{2,1,0:T(8,128)S(1)} fusion(f32[1024,16,4]{0,1,2:T(8,128)S(1)} %fusion.71, f32[1024,16,4]{0,1,2:T(8,128)S(1)} %all_to_all.127), kind=kOutput, calls=%fused_computation.55 | convolution fusion | flops 820051968 | bytes 786432 | tf_op jit(solution)/shard_map/xkz,xm->zkm/dot_general | solution.py:62
  274.7 9.8 %all-to-all-start.7 = ((f32[32,1,2048]{2,1,0:T(1,128)}), f32[32,1,2048]{2,1,0:T(1,128)S(1)}, u32[]{:S(2)}, u32[]{:S(2)}) async-start(f32[32,1,2048]{2,1,0:T(1,128)} %reshape.228), calls=%async_computation.7 | async-start | bytes 524288 | tf_op jit(solution)/shard_map/all_to_all | solution.py:112
  284.5 18.4 %fusion.59 = f32[4,16,1024]{2,1,0:T(8,128)S(1)} fusion(f32[1024,16,4]{0,1,2:T(8,128)S(1)} %fusion.68, f32[1024,16,4]{0,1,2:T(8,128)S(1)} %all_to_all.123), kind=kOutput, calls=%fused_computation.53 | convolution fusion | flops 820051968 | bytes 786432 | tf_op jit(solution)/shard_map/xkz,xm->zkm/dot_general | solution.py:62
  306.0 9.7 %all-to-all-start.6 = ((f32[32,1,2048]{2,1,0:T(1,128)}), f32[32,1,2048]{2,1,0:T(1,128)}, u32[]{:S(2)}, u32[]{:S(2)}) async-start(f32[32,1,2048]{2,1,0:T(1,128)} %reshape.230), calls=%async_computation.6 | async-start | bytes 524288 | tf_op jit(solution)/shard_map/all_to_all | solution.py:111
  340.8 6.1 collective-permute-start
  346.9 16.3 %scatter_fusion = f32[4,32,1024]{2,1,0:T(8,128)S(1)} fusion(f32[4,32,1024]{2,1,0:T(8,128)S(1)} %copy-done, s32[256]{0:T(256)S(1)} %bitcast.186, f32[256]{0:T(256)S(1)} %copy-done.10), kind=kCustom, calls=%fused_computation | custom fusion | flops 256 | bytes 6144 | tf_op jit(solution)/shard_map/scatter-add | solution.py:153
  393.4 102.6 %all-reduce.8 = (f32[]{:T(128)}, f32[]{:T(128)}) all-reduce(f32[]{:T(128)} %get-tuple-element.4, f32[]{:T(128)} %get-tuple-element.3), channel_id=1, replica_groups=mesh['gx'=32,'gy'=16] {'gx','gy'}, use_global_device_ids=true, to_apply=%region_2.3 | all-reduce | flops 2 | bytes 16 | tf_op jit(solution)/shard_map/psum | solution.py:158
  500.2 95.3 %psum.44 = f32[]{:T(128)} all-reduce(f32[]{:T(128)} %get-tuple-element.14), channel_id=1, replica_groups=mesh['gx'=32,'gy'=16] {'gx','gy'}, use_global_device_ids=true, to_apply=%region_6.7 | all-reduce | flops 1 | bytes 8 | tf_op jit(solution)/shard_map/psum | solution.py:158
  616.7 99.7 %psum.45 = f32[]{:T(128)} all-reduce(f32[]{:T(128)} %get-tuple-element.12), channel_id=1, replica_groups=mesh['gx'=32,'gy'=16] {'gx','gy'}, use_global_device_ids=true, to_apply=%region_8.9 | all-reduce | flops 1 | bytes 8 | tf_op jit(solution)/shard_map/psum | solution.py:158
  720.9 96.3 %psum.46 = f32[]{:T(128)} all-reduce(f32[]{:T(128)} %get-tuple-element.9), channel_id=1, replica_groups=mesh['gx'=32,'gy'=16] {'gx','gy'}, use_global_device_ids=true, to_apply=%region_10.11 | all-reduce | flops 1 | bytes 8 | tf_op jit(solution)/shard_map/psum | solution.py:158
  838.5 99.1 %psum.47 = f32[]{:T(128)} all-reduce(f32[]{:T(128)} %get-tuple-element.7), channel_id=1, replica_groups=mesh['gx'=32,'gy'=16] {'gx','gy'}, use_global_device_ids=true, to_apply=%region_12.13 | all-reduce | flops 1 | bytes 8 | tf_op jit(solution)/shard_map/psum | solution.py:158
  (153 shorter events, 168.6 us)
Async XLA Ops:
  21.5 38.2 %all-to-all-start.1 = ((f32[32,1,2048]{2,1,0:T(1,128)}), f32[32,1,2048]{2,1,0:T(1,128)S(1)}, u32[]{:S(2)}, u32[]{:S(2)}) async-start(f32[32,1,2048]{2,1,0:T(1,128)} %reshape.216), calls=%async_computation.1 | async-start | bytes 524288 | tf_op jit(solution)/shard_map/all_to_all | solution.py:112
  59.6 30.9 %all-to-all-start = ((f32[32,1,2048]{2,1,0:T(1,128)}), f32[32,1,2048]{2,1,0:T(1,128)S(1)}, u32[]{:S(2)}, u32[]{:S(2)}) async-start(f32[32,1,2048]{2,1,0:T(1,128)} %reshape.218), calls=%async_computation | async-start | bytes 524288 | tf_op jit(solution)/shard_map/all_to_all | solution.py:111
  133.0 30.4 %all-to-all-start.2 = ((f32[16,1,4096]{2,1,0:T(1,128)}), f32[16,1,4096]{2,1,0:T(1,128)S(1)}, u32[]{:S(2)}, u32[]{:S(2)}) async-start(f32[16,1,4096]{2,1,0:T(1,128)} %reshape.220), calls=%async_computation.2 | async-start | bytes 524288 | tf_op jit(solution)/shard_map/all_to_all | solution.py:117
  163.4 19.0 %all-to-all-start.3 = ((f32[16,1,4096]{2,1,0:T(1,128)}), f32[16,1,4096]{2,1,0:T(1,128)S(1)}, u32[]{:S(2)}, u32[]{:S(2)}) async-start(f32[16,1,4096]{2,1,0:T(1,128)} %reshape.222), calls=%async_computation.3 | async-start | bytes 524288 | tf_op jit(solution)/shard_map/all_to_all | solution.py:118
  192.3 15.9 %all-to-all-start.4 = ((f32[16,1,4096]{2,1,0:T(1,128)}), f32[16,1,4096]{2,1,0:T(1,128)S(1)}, u32[]{:S(2)}, u32[]{:S(2)}) async-start(f32[16,1,4096]{2,1,0:T(1,128)} %reshape.224), calls=%async_computation.4 | async-start | bytes 524288 | tf_op jit(solution)/shard_map/all_to_all | solution.py:117
  208.2 24.2 %all-to-all-start.5 = ((f32[16,1,4096]{2,1,0:T(1,128)}), f32[16,1,4096]{2,1,0:T(1,128)S(1)}, u32[]{:S(2)}, u32[]{:S(2)}) async-start(f32[16,1,4096]{2,1,0:T(1,128)} %reshape.226), calls=%async_computation.5 | async-start | bytes 524288 | tf_op jit(solution)/shard_map/all_to_all | solution.py:118
  274.7 31.3 %all-to-all-start.7 = ((f32[32,1,2048]{2,1,0:T(1,128)}), f32[32,1,2048]{2,1,0:T(1,128)S(1)}, u32[]{:S(2)}, u32[]{:S(2)}) async-start(f32[32,1,2048]{2,1,0:T(1,128)} %reshape.228), calls=%async_computation.7 | async-start | bytes 524288 | tf_op jit(solution)/shard_map/all_to_all | solution.py:112
  306.0 19.3 %all-to-all-start.6 = ((f32[32,1,2048]{2,1,0:T(1,128)}), f32[32,1,2048]{2,1,0:T(1,128)}, u32[]{:S(2)}, u32[]{:S(2)}) async-start(f32[32,1,2048]{2,1,0:T(1,128)} %reshape.230), calls=%async_computation.6 | async-start | bytes 524288 | tf_op jit(solution)/shard_map/all_to_all | solution.py:111
  339.5 23.7 %collective-permute-start.1 = (f32[4,1,1024]{2,1,0:T(1,128)S(1)}, f32[4,1,1024]{2,1,0:T(1,128)S(1)}, u32[]{:S(2)}, u32[]{:S(2)}) collective-permute-start(f32[4,1,1024]{2,1,0:T(1,128)S(1)} %get-tuple-element.45), channel_id=1, source_target_pairs={{16,0},{32,16},{48,32},{64,48},{80,64},{96,80},{112,96},{128,112},... | collective-permute-start | bytes 49160 | tf_op jit(solution)/shard_map/ppermute | solution.py:26
  340.8 22.4 %collective-permute-start = (f32[4,1,1024]{2,1,0:T(1,128)S(1)}, f32[4,1,1024]{2,1,0:T(1,128)S(1)}, u32[]{:S(2)}, u32[]{:S(2)}) collective-permute-start(f32[4,1,1024]{2,1,0:T(1,128)S(1)} %get-tuple-element.44), channel_id=1, source_target_pairs={{0,16},{16,32},{32,48},{48,64},{64,80},{80,96},{96,112},{112,128},... | collective-permute-start | bytes 49160 | tf_op jit(solution)/shard_map/ppermute | solution.py:23
  363.2 7.9 collective-permute-start.3
  367.3 5.0 collective-permute-start.2
  375.0 5.3 collective-permute-start.5
  376.3 4.8 collective-permute-start.4
  381.2 8.5 collective-permute-start.7
  383.2 7.8 collective-permute-start.6
  598.0 5.3 collective-permute-start.9
  599.3 4.8 collective-permute-start.8
  604.2 9.0 collective-permute-start.11
  607.9 6.5 collective-permute-start.10
  819.8 5.3 collective-permute-start.13
  821.1 4.8 collective-permute-start.12
  826.0 9.0 collective-permute-start.15
  829.7 6.5 collective-permute-start.14
  (12 other events, 411.9 us)
where the time goes:
time: 954 us; the launch traced here: 942 us
  blocking collectives  493 us (52%)
  matrix products  166 us (17%)
  starting transfers between devices  121 us (13%)
  other arithmetic  81.6 us (9%)
  local copies, waits for them, and re-layouts  40 us (4%)
  waiting for transfers between devices  28.4 us (3%)
  between operations  12.4 us (1%)
    psum x5, blocking collectives, global_dot(): return lax.psum(jnp.sum(first * second), ('gx', 'gy'))  493 us
    dot_general x20, matrix products, contract(): jnp.einsum(form, data, table, precision=HIGHEST, preferred_element_type=j...  166 us
    ppermute x8, starting transfers between devices, padded_2(): lax.ppermute(lax.slice_in_dim(block, block.shape[dim] - width, None, axis...  34.8 us
    unnamed x40, local copies, waits for them, and re-layouts  25.3 us
    all_to_all x2, starting transfers between devices, across_gx(): lax.all_to_all(pair[1], 'gx', split_axis=2, concat_axis=1, tiled=True)  23.5 us
    all_to_all x2, starting transfers between devices, across_gx(): lax.all_to_all(pair[0], 'gx', split_axis=2, concat_axis=1, tiled=True)  19.1 us
  transfers between devices with their start and end apart: 24, of which 14 were waited for; matrix products, arithmetic and copies ran while one was open for 14% of the time, Pallas kernels for 0%

commit v1 on v0

v1 whole, which is shorter than its diff:
```python
import math

import jax
import jax.numpy as jnp
import numpy as np
from jax import lax
from jax.experimental import pallas as pl
from jax.experimental.pallas import tpu as pltpu
from jax.sharding import PartitionSpec as P

AMPLITUDE = 4.0
BF16 = jnp.bfloat16
F32 = jnp.float32
INTERPRET = False


def call(body, outs, *args, specs=None):
    return pl.pallas_call(
        body,
        out_shape=outs,
        in_specs=specs or [pl.BlockSpec(memory_space=pltpu.VMEM)] * len(args),
        interpret=INTERPRET,
        compiler_params=pltpu.CompilerParams(vmem_limit_bytes=60 * 2**20),
    )(*args)


def f32(*shape):
    return jax.ShapeDtypeStruct(shape, F32)


def halves(table):
    high = table.astype(BF16)
    low = (table - high.astype(np.float64)).astype(BF16)
    return jnp.asarray(high), jnp.asarray(low)


def cosine_sine(product, length):
    angle = (product % length).astype(np.float64) * (2.0 * math.pi / length)
    return np.cos(angle), np.sin(angle)


def table_y(length):
    half = length // 2
    k = np.concatenate([np.arange(0, half, 2), np.arange(1, half, 2)])
    cos, sin = cosine_sine(k[:, None] * np.arange(half)[None, :], length)
    return np.stack([cos, -sin], axis=1).reshape(2 * half, half)


def tables_zx(gx, gy, zl, xl):
    row_x, row_z = np.repeat(np.arange(gx), gy), np.tile(np.arange(gy), gx)
    col_x, col_z = np.tile(np.arange(xl), zl), np.repeat(np.arange(zl), xl)

    def table(left_x, right_x, left_z, right_z, size_x, size_z):
        phase = np.outer(left_x, right_x) / size_x + np.outer(left_z, right_z) / size_z
        return np.exp(-2j * math.pi * phase)

    outer = table(row_x, row_x, row_z, row_z, gx, gy)
    twiddle = table(row_x, col_x, row_z, col_z, gx * xl, gy * zl)
    inner = table(col_x, col_x, col_z, col_z, xl, zl)
    forward = np.block([[inner.real, inner.imag], [-inner.imag, inner.real]])
    return outer, twiddle, forward


def split(data):
    high = data.astype(BF16)
    return high, (data - high.astype(F32)).astype(BF16)


def dot(a, b):
    return jnp.dot(a, b, preferred_element_type=F32)


def left_product(table, data):
    (th, tl), (dh, dl) = table, data
    return dot(th, dh) + (dot(th, dl) + dot(tl, dh))


def right_product(data, table):
    (dh, dl), (th, tl) = data, table
    return dot(dh, th) + (dot(dl, th) + dot(dh, tl))


def mix_bits(seed_rows, cells):
    shift = lax.shift_right_logical
    hashed = seed_rows + cells * jnp.int32(-1640531535)
    hashed = hashed ^ shift(hashed, jnp.int32(16))
    hashed = hashed * jnp.int32(-2048144789)
    hashed = hashed ^ shift(hashed, jnp.int32(13))
    hashed = hashed * jnp.int32(-1028477387)
    hashed = hashed ^ shift(hashed, jnp.int32(16))
    value = shift(hashed, jnp.int32(8)).astype(F32)
    return (value + 0.5) * (2.0 * math.sqrt(3.0) / 16777216.0) - math.sqrt(3.0)


def noise_kernel(seed_ref, th_ref, tl_ref, out_ref):
    rows, half = th_ref.shape
    seeds = seed_ref[...]
    cells = lax.broadcasted_iota(jnp.int32, (half, seeds.shape[1]), 0)
    near = mix_bits(seeds, cells)
    far = mix_bits(seeds, cells + half)
    mid = rows // 2
    out_ref[:mid] = left_product((th_ref[:mid], tl_ref[:mid]), split(near + far))
    out_ref[mid:] = left_product((th_ref[mid:], tl_ref[mid:]), split(near - far))


def power(base, exponent):
    return jnp.exp(exponent * jnp.log(base))


def spectrum_kernel(sizes, device_ref, lengths_ref, exponents_ref, data_ref, ar_h, ar_l, ai_h, ai_l, tr_ref, ti_ref, fh_ref, fl_ref, gh_ref, gl_ref, out_ref):
    gx, gy, zl, xl, length_y = sizes
    rows, cols = gx * gy, zl * xl
    outer_r = (ar_h[...], ar_l[...])
    outer_i = (ai_h[...], ai_l[...])
    tr, ti = tr_ref[...], ti_ref[...]
    shape = (rows, cols)
    row = lax.broadcasted_iota(jnp.int32, shape, 0)
    col = lax.broadcasted_iota(jnp.int32, shape, 1)
    kx = lax.div(row, gy) + gx * lax.rem(col, xl)
    kz = lax.rem(row, gy) + gy * lax.div(col, xl)
    device = device_ref[0]
    half_rows = rows // 2
    ky = jnp.where(device < half_rows, 2 * device, 2 * (device - half_rows) + 1)

    def wave(index, length):
        folded = jnp.minimum(index, length - index)
        return folded.astype(F32) * (2.0 * math.pi / length)

    ky_all = jnp.full((8, cols), ky, jnp.int32)
    total_y = 1.0 + power(lengths_ref[2] * wave(ky_all, length_y), exponents_ref[2])
    weight = jnp.where(ky_all == 0, 1.0, 2.0)
    volume = jnp.full((8, cols), lengths_ref[0] * lengths_ref[1] * lengths_ref[2], F32)
    scale = 1.0 / (gx * xl * gy * zl * length_y)
    numerator = AMPLITUDE * jnp.sqrt(volume) * scale * weight
    total = power(lengths_ref[0] * wave(kz, gy * zl), exponents_ref[0])
    total = total + power(lengths_ref[1] * wave(kx, gx * xl), exponents_ref[1])
    gain = numerator[:1] / (total_y[:1] + total)
    data = jnp.concatenate([data_ref[pl.ds(0, rows, stride=2), :], data_ref[pl.ds(1, rows, stride=2), :]], axis=1)
    parts = split(data)
    pr, pi = left_product(outer_r, parts), left_product(outer_i, parts)
    yr, yi = pr[:, :cols] - pi[:, cols:], pr[:, cols:] + pi[:, :cols]
    data = jnp.concatenate([yr * tr - yi * ti, yr * ti + yi * tr], axis=1)
    data = right_product(split(data), (fh_ref[...], fl_ref[...]))
    data = data * jnp.concatenate([gain, gain], axis=1)
    data = right_product(split(data), (gh_ref[...], gl_ref[...]))
    yr, yi = data[:, :cols], data[:, cols:]
    data = jnp.concatenate([yr * tr + yi * ti, yi * tr - yr * ti], axis=1)
    parts = split(data)
    pr, pi = left_product(outer_r, parts), left_product(outer_i, parts)
    out_ref[pl.ds(0, rows, stride=2), :] = pr[:, :cols] + pi[:, cols:]
    out_ref[pl.ds(1, rows, stride=2), :] = pr[:, cols:] - pi[:, :cols]


def faces(value, xl, refs):
    rows = value.shape[0]
    refs[0][...] = value[:xl]
    refs[1][...] = value[rows - xl :]
    for layer in range(rows // xl):
        refs[2][layer : layer + 1] = value[layer * xl : layer * xl + 1]
        refs[3][layer : layer + 1] = value[(layer + 1) * xl - 1 : (layer + 1) * xl]


def field_kernel(xl, data_ref, th_ref, tl_ref, log_ref, perm_ref, *face_refs):
    rows, half = th_ref.shape
    mid = rows // 2
    turned = jnp.transpose(data_ref[...])
    even = right_product(split(turned[:, :mid]), (th_ref[:mid], tl_ref[:mid]))
    odd = right_product(split(turned[:, mid:]), (th_ref[mid:], tl_ref[mid:]))
    log_ref[:, :half] = even + odd
    log_ref[:, half:] = even - odd
    perm = jnp.exp(log_ref[...])
    perm_ref[...] = perm
    faces(perm, xl, face_refs)


def shifted(value, halo, xl):
    z_low, z_high, x_low, x_high = halo
    rows, length = value.shape
    layers = rows // xl
    place = lax.broadcasted_iota(jnp.int32, (xl, length), 0)
    lows, highs = [], []
    for layer in range(layers):
        block = value[layer * xl : (layer + 1) * xl]
        lows.append(jnp.where(place == 0, x_low[layer : layer + 1], pltpu.roll(block, 1, 0)))
        highs.append(jnp.where(place == xl - 1, x_high[layer : layer + 1], pltpu.roll(block, xl - 1, 0)))
    return (
        jnp.concatenate([z_low, value[: rows - xl]], axis=0),
        jnp.concatenate([value[xl:], z_high], axis=0),
        jnp.concatenate(lows, axis=0),
        jnp.concatenate(highs, axis=0),
        pltpu.roll(value, 1, 1),
        pltpu.roll(value, length - 1, 1),
    )


def lane_sum(value, lane_at):
    total = jnp.sum(jnp.sum(value, axis=0, keepdims=True), axis=1, keepdims=True)
    lane = lax.broadcasted_iota(jnp.int32, (1, 128), 1)
    return jnp.where(lane == lane_at, total, 0.0)


def rhs_kernel(origin_ref, recharge_ref, cells_ref, rates_ref, rhs_ref, *, xl):
    rows, length = recharge_ref.shape
    wells = cells_ref.shape[1]
    layer = cells_ref[0:1] - origin_ref[0]
    line = cells_ref[1:2] - origin_ref[1]
    inside = (line >= 0) & (line < xl)
    at = jnp.where(inside, layer * xl + line, -1)
    rate = jnp.where(lax.broadcasted_iota(jnp.int32, (rows, wells), 0) == at, rates_ref[...], 0.0)
    column = (lax.broadcasted_iota(jnp.int32, (length, wells), 0) == cells_ref[2:3]).astype(F32).astype(BF16)
    added = None
    for _ in range(3):
        part = rate.astype(BF16)
        rate = rate - part.astype(F32)
        product = lax.dot_general(part, column, (((1,), (1,)), ((), ())), preferred_element_type=F32)
        added = product if added is None else added + product
    rhs_ref[...] = recharge_ref[...] + added


def setup_kernel(xl, perm_ref, h0, h1, h2, h3, storage_ref, rhs_ref, c0, c1, c2, c3, c4, c5, diag_ref, u_ref, f0, f1, f2, f3, mom_ref):
    perm = perm_ref[...]
    length = perm.shape[1]
    place = lax.broadcasted_iota(jnp.int32, perm.shape, 1)
    around = list(shifted(perm, (h0[...], h1[...], h2[...], h3[...]), xl))
    around[4] = jnp.where(place == 0, 0.0, around[4])
    around[5] = jnp.where(place == length - 1, 0.0, around[5])
    twice = 2.0 * perm
    flows = [twice * other / (perm + other) for other in around]
    diag = storage_ref[...]
    for flow in flows:
        diag = diag + flow
    inverse = 1.0 / diag
    for ref, flow in zip((c0, c1, c2, c3, c4, c5), flows):
        ref[...] = flow * inverse
    rhs = rhs_ref[...]
    u = rhs * inverse
    diag_ref[...] = diag
    u_ref[...] = u
    faces(u, xl, (f0, f1, f2, f3))
    mom_ref[...] = lane_sum(rhs * u, 0)


def step_kernel(xl, at, last, u_ref, h0, h1, h2, h3, c0, c1, c2, c3, c4, c5, diag_ref, mom_in, new_ref, *rest):
    around = shifted(u_ref[...], (h0[...], h1[...], h2[...], h3[...]), xl)
    new = None
    for coef, other in zip((c0, c1, c2, c3, c4, c5), around):
        term = coef[...] * other
        new = term if new is None else new + term
    new_ref[...] = new
    weighted = diag_ref[...] * new
    mom = mom_in[...] + lane_sum(weighted * u_ref[...], at)
    if last:
        rest[0][...] = jnp.broadcast_to(mom, rest[0].shape)
    else:
        faces(new, xl, rest[:4])
        rest[4][...] = mom + lane_sum(weighted * new, at + 1)


def partial_kernel(in_ref, out_ref):
    out_ref[...] = jnp.broadcast_to(jnp.sum(in_ref[...], axis=0, keepdims=True), out_ref.shape)


def final_kernel(iters, mom_ref, u0, u1, u2, u3, diag_ref, pressure_ref, residual_ref):
    moments = jnp.sum(mom_ref[...], axis=0, keepdims=True)
    lane = lax.broadcasted_iota(jnp.int32, (1, 128), 1)
    nu = [jnp.sum(jnp.where(lane == i, moments, 0.0), axis=1, keepdims=True) for i in range(2 * iters)]

    def form(a, b):
        total = None
        for i, left in enumerate(a):
            for j, right in enumerate(b):
                term = left * right * nu[i + j]
                total = term if total is None else total + term
        return total

    one = jnp.ones((1, 1), F32)
    zero = jnp.zeros((1, 1), F32)
    precond, direction, pressure = [one], [one], [zero] * iters
    rz = nu[0]
    for it in range(iters):
        image = [
            (direction[i] if i < len(direction) else zero) - (direction[i - 1] if i > 0 else zero)
            for i in range(len(direction) + 1)
        ]
        alpha = rz / form(direction, image)
        pressure = [old + alpha * direction[i] if i < len(direction) else old for i, old in enumerate(pressure)]
        precond = [(precond[i] if i < len(precond) else zero) - alpha * image[i] for i in range(len(image))]
        if it + 1 < iters:
            new = form(precond, precond)
            beta = new / rz
            direction = [
                precond[i] + beta * direction[i] if i < len(direction) else precond[i] for i in range(len(precond))
            ]
            rz = new
    basis = [u0[...], u1[...], u2[...], u3[...]]
    pressure_ref[...] = pressure[0] * basis[0] + pressure[1] * basis[1] + pressure[2] * basis[2]
    total = precond[0] * basis[0] + precond[1] * basis[1] + precond[2] * basis[2] + precond[3] * basis[3]
    residual_ref[...] = diag_ref[...] * total


ITERS = 3


def exchange(face):
    out = []
    for axis, low, high in (("gy", face[0], face[1]), ("gx", face[2], face[3])):
        count = lax.axis_size(axis)
        up = [(i, i + 1) for i in range(count - 1)]
        down = [(i + 1, i) for i in range(count - 1)]
        out.append(lax.ppermute(high, axis, up))
        out.append(lax.ppermute(low, axis, down))
    return out


def shards(seeds, lengths, exponents, storage, recharge, well_cells, well_rates):
    zl, xl, length_y = storage.shape
    gx, gy = lax.axis_size("gx"), lax.axis_size("gy")
    rows = zl * xl
    block, zface, xface = f32(rows, length_y), f32(xl, length_y), f32(zl, length_y)
    face_shapes = [zface, zface, xface, xface]
    at_x, at_y = lax.axis_index("gx"), lax.axis_index("gy")
    device = (at_x * gy + at_y).reshape(1).astype(jnp.int32)
    origin = jnp.stack([at_y * zl, at_x * xl]).astype(jnp.int32)
    smem = pl.BlockSpec(memory_space=pltpu.SMEM)
    vmem = pl.BlockSpec(memory_space=pltpu.VMEM)
    ty = halves(table_y(length_y))
    outer, twiddle, inner = tables_zx(gx, gy, zl, xl)

    spectrum = call(noise_kernel, f32(length_y, rows), seeds.reshape(1, rows), *ty)
    rhs = call(
        lambda *refs: rhs_kernel(*refs, xl=xl),
        block,
        origin,
        recharge.reshape(rows, length_y),
        well_cells,
        well_rates.reshape(1, -1),
        specs=[smem, vmem, vmem, vmem],
    )

    def everywhere(array):
        return lax.all_to_all(array, ("gx", "gy"), split_axis=0, concat_axis=0, tiled=True)

    spectrum = everywhere(spectrum)
    spectrum = call(
        lambda *refs: spectrum_kernel((gx, gy, zl, xl, length_y), *refs),
        f32(length_y, rows),
        device,
        lengths,
        exponents,
        spectrum,
        *halves(outer.real),
        *halves(outer.imag),
        jnp.asarray(twiddle.real, F32),
        jnp.asarray(twiddle.imag, F32),
        *halves(inner),
        *halves(inner.T),
        specs=[smem, smem, smem] + [vmem] * 11,
    )
    spectrum = everywhere(spectrum)
    log_perm, perm, *face = call(
        lambda *refs: field_kernel(xl, *refs), [block, block] + face_shapes, spectrum, *ty
    )
    *coefs, diag, u0, f0, f1, f2, f3, moments = call(
        lambda *refs: setup_kernel(xl, *refs),
        [block] * 8 + face_shapes + [f32(1, 128)],
        perm,
        *exchange(face),
        storage.reshape(rows, length_y),
        rhs,
    )
    face = (f0, f1, f2, f3)
    basis = [u0]
    for step in range(ITERS):
        last = step + 1 == ITERS
        outs = [block, f32(gx, 128)] if last else [block] + face_shapes + [f32(1, 128)]
        new, *rest = call(
            lambda *refs, step=step, last=last: step_kernel(xl, 2 * step + 1, last, *refs),
            outs,
            basis[-1],
            *exchange(face),
            *coefs,
            diag,
            moments,
        )
        basis.append(new)
        face, moments = rest[:4], rest[-1]
    moments = lax.all_to_all(moments, "gx", split_axis=0, concat_axis=0, tiled=True)
    moments = call(partial_kernel, f32(gy, 128), moments)
    moments = lax.all_to_all(moments, "gy", split_axis=0, concat_axis=0, tiled=True)
    pressure, residual = call(
        lambda *refs: final_kernel(ITERS, *refs), [block, block], moments, *basis, diag
    )
    shape = storage.shape
    return (log_perm.reshape(shape), pressure.reshape(shape), residual.reshape(shape))


def solution(mesh):
    placed = (P("gy", "gx"), P(), P(), P("gy", "gx", None), P("gy", "gx", None), P(), P())
    return jax.shard_map(
        shards,
        mesh=mesh,
        in_specs=placed,
        out_specs=(P("gy", "gx", None), P("gy", "gx", None), P("gy", "gx", None)),
        check_vma=False,
    )
```

time: 954 us -> 211 us (0.22); the launches traced: 942 us -> 210 us
  blocking collectives: 493 us -> 70.7 us
  matrix products: 166 us -> 0 us
  other arithmetic: 81.6 us -> 0.61 us
  starting transfers between devices: 121 us -> 65.3 us
  local copies, waits for them, and re-layouts: 40 us -> 4.8 us
  Pallas kernels: 0 us -> 35 us
  between operations: 12.4 us -> 0.93 us
    psum x5 -> x0, blocking collectives: 493 us -> none  [global_dot(): return lax.psum(jnp.sum(first * second), ('gx', 'gy'))]
    dot_general x20 -> x0, matrix products: 166 us -> none  [contract(): jnp.einsum(form, data, table, precision=HIGHEST, preferred_element_type=j...]
    all_to_all x0 -> x3, blocking collectives: none -> 70.7 us  [the longest x1 33.1 us: everywhere(): lax.all_to_all(array, ('gx', 'gy'), split_axis=0, concat_axis=0, tiled=True)]
    all_to_all x8 -> x1, starting transfers between devices: 67.3 us -> 22.2 us  [everywhere(): lax.all_to_all(array, ('gx', 'gy'), split_axis=0, concat_axis=0, tiled=True)]
    pallas_call x0 -> x10, Pallas kernels: none -> 35 us  [call(): pl.pallas_call(body, out_shape=outs, in_specs=specs or [pl.BlockSpec(memo...]
    unnamed x40 -> x34, local copies, waits for them, and re-layouts: 25.3 us -> 3.53 us
    scatter-add x1 -> x0, other arithmetic: 16.3 us -> none  [shards(): recharge.at[local_layer, local_row, well_cells[2]]]
    sin x1 -> x0, other arithmetic: 15.6 us -> none  [dft_tables(): return (jnp.cos(angle), jnp.sin(angle))]
  transfers between devices with their start and end apart: 24 -> 17, of which waited for: 14 -> 5; matrix products, arithmetic and copies ran while one was open for 14% -> 0% of each run, Pallas kernels for 0% -> 1%
where the time goes in v1:
time: 211 us; the launch traced here: 210 us
  blocking collectives  70.7 us (34%)
  starting transfers between devices  65.3 us (31%)
  Pallas kernels  35 us (17%)
  waiting for transfers between devices  32.5 us (15%)
  local copies, waits for them, and re-layouts  4.8 us (2%)
    pallas_call x10, Pallas kernels, call(): pl.pallas_call(body, out_shape=outs, in_specs=specs or [pl.BlockSpec(memo...  35 us
    all_to_all x1, blocking collectives, everywhere(): lax.all_to_all(array, ('gx', 'gy'), split_axis=0, concat_axis=0, tiled=True)  33.1 us
    ppermute x8, starting transfers between devices, exchange(): out.append(lax.ppermute(high, axis, up))  30.2 us
    all_to_all x1, starting transfers between devices, everywhere(): lax.all_to_all(array, ('gx', 'gy'), split_axis=0, concat_axis=0, tiled=True)  22.2 us
    all_to_all x1, waiting for transfers between devices, everywhere(): lax.all_to_all(array, ('gx', 'gy'), split_axis=0, concat_axis=0, tiled=True)  21.9 us
    all_to_all x1, blocking collectives, shards(): lax.all_to_all(moments, 'gx', split_axis=0, concat_axis=0, tiled=True)  19.1 us
    all_to_all x1, blocking collectives, shards(): lax.all_to_all(moments, 'gy', split_axis=0, concat_axis=0, tiled=True)  18.5 us
    ppermute x8, starting transfers between devices, exchange(): out.append(lax.ppermute(low, axis, down))  13 us
  transfers between devices with their start and end apart: 17, of which 5 were waited for; matrix products, arithmetic and copies ran while one was open for 0% of the time, Pallas kernels for 1%

profile of v1, /device:TPU:1, one launch (start us, length us, event | category | flops | bytes accessed | tf_op | source)
XLA Modules:
  0.0 209.8 jit_solution(13088498437514661531)
XLA Ops:
  1.9 3.5 %shard_map.202 = f32[1024,128]{1,0:T(8,128)} custom-call(s32[1,128]{1,0:T(1,128)} %reshape.39.seed_ref, bf16[1024,512]{1,0:T(8,128)(2,1)} %constant.39.clone.th_ref.refs_1_, bf16[1024,512]{1,0:T(8,128)(2,1)} %constant.40.clone.tl_ref.refs_2_), custom_call_target="tpu_custom_call" | custom-call | tf_op jit(solution)/shard_map/pallas_call | solution.py:18
  5.4 22.2 %all-to-all-start = ((f32[512,2,128]{2,1,0:T(2,128)}), f32[512,2,128]{2,1,0:T(2,128)S(1)}, u32[]{:S(2)}, u32[]{:S(2)}) async-start(f32[512,2,128]{2,1,0:T(2,128)} %bitcast.24), calls=%async_computation | async-start | bytes 1048576 | tf_op jit(solution)/shard_map/all_to_all | solution.py:341
  27.6 21.9 %all-to-all-done = f32[512,2,128]{2,1,0:T(2,128)S(1)} async-done(((f32[512,2,128]{2,1,0:T(2,128)}), f32[512,2,128]{2,1,0:T(2,128)S(1)}, u32[]{:S(2)}, u32[]{:S(2)}) %all-to-all-start) | async-done | bytes 524320 | tf_op jit(solution)/shard_map/all_to_all | solution.py:341
  50.3 5.5 %shard_map.203 = f32[1024,128]{1,0:T(8,128)} custom-call(s32[1]{0:T(128)} %bitcast.refs_0_, f32[3]{0:T(128)} %refs_1_.2, f32[3]{0:T(128)} %refs_2_.3, f32[1024,128]{1,0:T(8,128)} %bitcast.21, bf16[512,512]{1,0:T(8,128)(2,1)} %constant.41.clone.refs_4_, bf16[512,512]{1,0:T(8,128)(2,1)} %constant.42.clone.refs_5_, bf16[512,512]{1,0:T(8,128)(2,1)} %constant.43.clone.refs_6_, ...), custom_call_target="tpu_custom_call" | custom-call | tf_op jit(solution)/shard_map/pallas_call | solution.py:18
  55.8 33.1 %all_to_all.44 = f32[512,2,128]{2,1,0:T(2,128)} all-to-all(f32[512,2,128]{2,1,0:T(2,128)} %bitcast.22), channel_id=1, replica_groups=mesh['gx'=32,'gy'=16] {'gx','gy'}, dimensions={0} | all-to-all | bytes 1048576 | tf_op jit(solution)/shard_map/all_to_all | solution.py:341
  89.0 3.4 %shard_map.204 = (f32[128,1024]{1,0:T(8,128)}, f32[128,1024]{1,0:T(8,128)}, f32[32,1024]{1,0:T(8,128)}, f32[32,1024]{1,0:T(8,128)}, f32[4,1024]{1,0:T(4,128)}, /*index=5*/f32[4,1024]{1,0:T(4,128)}) custom-call(f32[1024,128]{1,0:T(8,128)} %bitcast.23, bf16[1024,512]{1,0:T(8,128)(2,1)} %constant.39.clone.th_ref.refs_1_, ...), custom_call_target="tpu_custom_call" | custom-call | tf_op jit(solution)/shard_map/pallas_call | solution.py:18
  92.4 3.5 %collective-permute-start = (f32[32,1024]{1,0:T(8,128)}, f32[32,1024]{1,0:T(8,128)S(1)}, u32[]{:S(2)}, u32[]{:S(2)}) collective-permute-start(f32[32,1024]{1,0:T(8,128)} %get-tuple-element.40), channel_id=1, source_target_pairs={{0,1},{1,2},{2,3},{3,4},{4,5},{5,6},{6,7},{7,8},{8,9},{9,10},{10,1... | collective-permute-start | bytes 393224 | tf_op jit(solution)/shard_map/ppermute | solution.py:310
  97.8 2.7 %collective-permute-start.2 = (f32[4,1024]{1,0:T(4,128)}, f32[4,1024]{1,0:T(4,128)S(1)}, u32[]{:S(2)}, u32[]{:S(2)}) collective-permute-start(f32[4,1024]{1,0:T(4,128)} %get-tuple-element.42), channel_id=1, source_target_pairs={{0,16},{16,32},{32,48},{48,64},{64,80},{80,96},{96,112},{112,128},... | collective-permute-start | bytes 49160 | tf_op jit(solution)/shard_map/ppermute | solution.py:310
  105.9 4.5 %shard_map.206 = (f32[128,1024]{1,0:T(8,128)}, f32[128,1024]{1,0:T(8,128)}, f32[128,1024]{1,0:T(8,128)}, f32[128,1024]{1,0:T(8,128)}, f32[128,1024]{1,0:T(8,128)...) custom-call(f32[128,1024]{1,0:T(8,128)} %get-tuple-element.39.refs_0, ...), custom_call_target="tpu_custom_call" | custom-call | tf_op jit(solution)/shard_map/pallas_call | solution.py:18
  110.5 5.1 %collective-permute-start.4 = (f32[32,1024]{1,0:T(8,128)}, f32[32,1024]{1,0:T(8,128)S(1)}, u32[]{:S(2)}, u32[]{:S(2)}) collective-permute-start(f32[32,1024]{1,0:T(8,128)} %get-tuple-element.45), channel_id=1, source_target_pairs={{0,1},{1,2},{2,3},{3,4},{4,5},{5,6},{6,7},{7,8},{8,9},{9,10},{10,1... | collective-permute-start | bytes 393224 | tf_op jit(solution)/shard_map/ppermute | solution.py:310
  117.5 2.9 %collective-permute-start.6 = (f32[4,1024]{1,0:T(4,128)}, f32[4,1024]{1,0:T(4,128)S(1)}, u32[]{:S(2)}, u32[]{:S(2)}) collective-permute-start(f32[4,1024]{1,0:T(4,128)} %get-tuple-element.47), channel_id=1, source_target_pairs={{0,16},{16,32},{32,48},{48,64},{64,80},{80,96},{96,112},{112,128},... | collective-permute-start | bytes 49160 | tf_op jit(solution)/shard_map/ppermute | solution.py:310
  121.6 3.4 %collective-permute-done.7.refs_4_ = f32[4,1024]{1,0:T(4,128)S(1)} collective-permute-done((f32[4,1024]{1,0:T(4,128)}, f32[4,1024]{1,0:T(4,128)S(1)}, u32[]{:S(2)}, u32[]{:S(2)}) %collective-permute-start.7) | collective-permute-done | bytes 16416 | tf_op jit(solution)/shard_map/ppermute | solution.py:311
  125.7 3.7 %shard_map.207 = (f32[128,1024]{1,0:T(8,128)}, f32[32,1024]{1,0:T(8,128)}, f32[32,1024]{1,0:T(8,128)}, f32[4,1024]{1,0:T(4,128)}, f32[4,1024]{1,0:T(4,128)}, /*index=5*/f32[1,128]{1,0:T(1,128)}) custom-call(f32[128,1024]{1,0:T(8,128)} %get-tuple-element.44.refs_0_.refs_1_, f32[32,1024]{1,0:T(8,128)} %copy-done.4, f32[32,1024]{1,0:T(8,128)} %copy-done.7, ...), custom_call_target="tpu_custom_call" | custom-call | tf_op jit(solution)/shard_map/pallas_call | solution.py:18
  129.5 5.1 %collective-permute-start.8 = (f32[32,1024]{1,0:T(8,128)}, f32[32,1024]{1,0:T(8,128)S(1)}, u32[]{:S(2)}, u32[]{:S(2)}) collective-permute-start(f32[32,1024]{1,0:T(8,128)} %get-tuple-element.58), channel_id=1, source_target_pairs={{0,1},{1,2},{2,3},{3,4},{4,5},{5,6},{6,7},{7,8},{8,9},{9,10},{10,1... | collective-permute-start | bytes 393224 | tf_op jit(solution)/shard_map/ppermute | solution.py:310
  136.5 2.7 %collective-permute-start.10 = (f32[4,1024]{1,0:T(4,128)}, f32[4,1024]{1,0:T(4,128)S(1)}, u32[]{:S(2)}, u32[]{:S(2)}) collective-permute-start(f32[4,1024]{1,0:T(4,128)} %get-tuple-element.60), channel_id=1, source_target_pairs={{0,16},{16,32},{32,48},{48,64},{64,80},{80,96},{96,112},{112,128},... | collective-permute-start | bytes 49160 | tf_op jit(solution)/shard_map/ppermute | solution.py:310
  140.7 3.2 %collective-permute-done.11.refs_4_ = f32[4,1024]{1,0:T(4,128)S(1)} collective-permute-done((f32[4,1024]{1,0:T(4,128)}, f32[4,1024]{1,0:T(4,128)S(1)}, u32[]{:S(2)}, u32[]{:S(2)}) %collective-permute-start.11) | collective-permute-done | bytes 16416 | tf_op jit(solution)/shard_map/ppermute | solution.py:311
  144.6 3.7 %shard_map.208 = (f32[128,1024]{1,0:T(8,128)}, f32[32,1024]{1,0:T(8,128)}, f32[32,1024]{1,0:T(8,128)}, f32[4,1024]{1,0:T(4,128)}, f32[4,1024]{1,0:T(4,128)}, /*index=5*/f32[1,128]{1,0:T(1,128)}) custom-call(f32[128,1024]{1,0:T(8,128)} %get-tuple-element.57.refs_0_.refs_2_, f32[32,1024]{1,0:T(8,128)} %copy-done.5, f32[32,1024]{1,0:T(8,128)} %copy-done.8, ...), custom_call_target="tpu_custom_call" | custom-call | tf_op jit(solution)/shard_map/pallas_call | solution.py:18
  148.3 5.1 %collective-permute-start.12 = (f32[32,1024]{1,0:T(8,128)}, f32[32,1024]{1,0:T(8,128)S(1)}, u32[]{:S(2)}, u32[]{:S(2)}) collective-permute-start(f32[32,1024]{1,0:T(8,128)} %get-tuple-element.64), channel_id=1, source_target_pairs={{0,1},{1,2},{2,3},{3,4},{4,5},{5,6},{6,7},{7,8},{8,9},{9,10},{10,1... | collective-permute-start | bytes 393224 | tf_op jit(solution)/shard_map/ppermute | solution.py:310
  155.3 3.2 %collective-permute-start.14 = (f32[4,1024]{1,0:T(4,128)}, f32[4,1024]{1,0:T(4,128)S(1)}, u32[]{:S(2)}, u32[]{:S(2)}) collective-permute-start(f32[4,1024]{1,0:T(4,128)} %get-tuple-element.66), channel_id=1, source_target_pairs={{0,16},{16,32},{32,48},{48,64},{64,80},{80,96},{96,112},{112,128},... | collective-permute-start | bytes 49160 | tf_op jit(solution)/shard_map/ppermute | solution.py:310
  159.8 3.7 %collective-permute-done.15.refs_4_ = f32[4,1024]{1,0:T(4,128)S(1)} collective-permute-done((f32[4,1024]{1,0:T(4,128)}, f32[4,1024]{1,0:T(4,128)S(1)}, u32[]{:S(2)}, u32[]{:S(2)}) %collective-permute-start.15) | collective-permute-done | bytes 16416 | tf_op jit(solution)/shard_map/ppermute | solution.py:311
  164.2 3.6 %shard_map.209 = (f32[128,1024]{1,0:T(8,128)}, f32[32,128]{1,0:T(8,128)}) custom-call(f32[128,1024]{1,0:T(8,128)} %get-tuple-element.63.refs_0_.refs_3_, f32[32,1024]{1,0:T(8,128)} %copy-done.3, f32[32,1024]{1,0:T(8,128)} %copy-done.6, f32[4,1024]{1,0:T(4,128)} %copy-done.11, f32[4,1024]{1,0:T(4,128)} %copy-done.14, f32[128,1024]{1,0:T(8,128)} %get-tuple-element.49.refs_5_, ...), custom_call_target="tpu_custom_call" | custom-call | tf_op jit(solution)/shard_map/pallas_call | solution.py:18
  167.8 19.1 %all_to_all.45 = f32[32,1,128]{2,1,0:T(1,128)} all-to-all(f32[32,1,128]{2,1,0:T(1,128)} %bitcast.30), channel_id=1, replica_groups=mesh['gx'=32,'gy'=16] {'gx'}, dimensions={0} | all-to-all | bytes 32768 | tf_op jit(solution)/shard_map/all_to_all | solution.py:387
  188.2 18.5 %all_to_all.46 = f32[16,1,128]{2,1,0:T(1,128)} all-to-all(f32[16,1,128]{2,1,0:T(1,128)} %bitcast.29), channel_id=1, replica_groups=mesh['gx'=32,'gy'=16] {'gy'}, dimensions={0} | all-to-all | bytes 16384 | tf_op jit(solution)/shard_map/all_to_all | solution.py:389
  206.7 3.1 %shard_map.211 = (f32[128,1024]{1,0:T(8,128)}, f32[128,1024]{1,0:T(8,128)}) custom-call(f32[16,128]{1,0:T(8,128)} %bitcast.28, f32[128,1024]{1,0:T(8,128)} %get-tuple-element.44.refs_0_.refs_1_, f32[128,1024]{1,0:T(8,128)} %get-tuple-element.57.refs_0_.refs_2_, f32[128,1024]{1,0:T(8,128)} %get-tuple-element.63.refs_0_.refs_3_, ...), custom_call_target="tpu_custom_call" | custom-call | tf_op jit(solution)/shard_map/pallas_call | solution.py:18
  (59 shorter events, 22.6 us)
Async XLA Ops:
  5.4 44.1 %all-to-all-start = ((f32[512,2,128]{2,1,0:T(2,128)}), f32[512,2,128]{2,1,0:T(2,128)S(1)}, u32[]{:S(2)}, u32[]{:S(2)}) async-start(f32[512,2,128]{2,1,0:T(2,128)} %bitcast.24), calls=%async_computation | async-start | bytes 1048576 | tf_op jit(solution)/shard_map/all_to_all | solution.py:341
  49.5 0.8 copy-start
  92.4 12.9 %collective-permute-start = (f32[32,1024]{1,0:T(8,128)}, f32[32,1024]{1,0:T(8,128)S(1)}, u32[]{:S(2)}, u32[]{:S(2)}) collective-permute-start(f32[32,1024]{1,0:T(8,128)} %get-tuple-element.40), channel_id=1, source_target_pairs={{0,1},{1,2},{2,3},{3,4},{4,5},{5,6},{6,7},{7,8},{8,9},{9,10},{10,1... | collective-permute-start | bytes 393224 | tf_op jit(solution)/shard_map/ppermute | solution.py:310
  95.9 9.4 %collective-permute-start.1 = (f32[32,1024]{1,0:T(8,128)}, f32[32,1024]{1,0:T(8,128)S(1)}, u32[]{:S(2)}, u32[]{:S(2)}) collective-permute-start(f32[32,1024]{1,0:T(8,128)} %get-tuple-element.41), channel_id=1, source_target_pairs={{1,0},{2,1},{3,2},{4,3},{5,4},{6,5},{7,6},{8,7},{9,8},{10,9},{11,1... | collective-permute-start | bytes 393224 | tf_op jit(solution)/shard_map/ppermute | solution.py:311
  97.8 7.2 %collective-permute-start.2 = (f32[4,1024]{1,0:T(4,128)}, f32[4,1024]{1,0:T(4,128)S(1)}, u32[]{:S(2)}, u32[]{:S(2)}) collective-permute-start(f32[4,1024]{1,0:T(4,128)} %get-tuple-element.42), channel_id=1, source_target_pairs={{0,16},{16,32},{32,48},{48,64},{64,80},{80,96},{96,112},{112,128},... | collective-permute-start | bytes 49160 | tf_op jit(solution)/shard_map/ppermute | solution.py:310
  100.5 4.7 %collective-permute-start.3 = (f32[4,1024]{1,0:T(4,128)}, f32[4,1024]{1,0:T(4,128)S(1)}, u32[]{:S(2)}, u32[]{:S(2)}) collective-permute-start(f32[4,1024]{1,0:T(4,128)} %get-tuple-element.43), channel_id=1, source_target_pairs={{16,0},{32,16},{48,32},{64,48},{80,64},{96,80},{112,96},{128,112},... | collective-permute-start | bytes 49160 | tf_op jit(solution)/shard_map/ppermute | solution.py:311
  105.2 0.7 copy-start.2
  110.5 14.6 %collective-permute-start.4 = (f32[32,1024]{1,0:T(8,128)}, f32[32,1024]{1,0:T(8,128)S(1)}, u32[]{:S(2)}, u32[]{:S(2)}) collective-permute-start(f32[32,1024]{1,0:T(8,128)} %get-tuple-element.45), channel_id=1, source_target_pairs={{0,1},{1,2},{2,3},{3,4},{4,5},{5,6},{6,7},{7,8},{8,9},{9,10},{10,1... | collective-permute-start | bytes 393224 | tf_op jit(solution)/shard_map/ppermute | solution.py:310
  115.5 9.5 %collective-permute-start.5 = (f32[32,1024]{1,0:T(8,128)}, f32[32,1024]{1,0:T(8,128)S(1)}, u32[]{:S(2)}, u32[]{:S(2)}) collective-permute-start(f32[32,1024]{1,0:T(8,128)} %get-tuple-element.46), channel_id=1, source_target_pairs={{1,0},{2,1},{3,2},{4,3},{5,4},{6,5},{7,6},{8,7},{9,8},{10,9},{11,1... | collective-permute-start | bytes 393224 | tf_op jit(solution)/shard_map/ppermute | solution.py:311
  117.5 4.2 %collective-permute-start.6 = (f32[4,1024]{1,0:T(4,128)}, f32[4,1024]{1,0:T(4,128)S(1)}, u32[]{:S(2)}, u32[]{:S(2)}) collective-permute-start(f32[4,1024]{1,0:T(4,128)} %get-tuple-element.47), channel_id=1, source_target_pairs={{0,16},{16,32},{32,48},{48,64},{64,80},{80,96},{96,112},{112,128},... | collective-permute-start | bytes 49160 | tf_op jit(solution)/shard_map/ppermute | solution.py:310
  120.3 4.7 %collective-permute-start.7 = (f32[4,1024]{1,0:T(4,128)}, f32[4,1024]{1,0:T(4,128)S(1)}, u32[]{:S(2)}, u32[]{:S(2)}) collective-permute-start(f32[4,1024]{1,0:T(4,128)} %get-tuple-element.48), channel_id=1, source_target_pairs={{16,0},{32,16},{48,32},{64,48},{80,64},{96,80},{112,96},{128,112},... | collective-permute-start | bytes 49160 | tf_op jit(solution)/shard_map/ppermute | solution.py:311
  121.6 3.4 %copy-start.12 = (f32[4,1024]{1,0:T(4,128)}, f32[4,1024]{1,0:T(4,128)S(1)}, u32[]{:S(2)}) copy-start(f32[4,1024]{1,0:T(4,128)S(1)} %collective-permute-done.6.refs_3_) | copy-start | bytes 49156
  125.0 0.7 copy-start.7
  129.5 14.4 %collective-permute-start.8 = (f32[32,1024]{1,0:T(8,128)}, f32[32,1024]{1,0:T(8,128)S(1)}, u32[]{:S(2)}, u32[]{:S(2)}) collective-permute-start(f32[32,1024]{1,0:T(8,128)} %get-tuple-element.58), channel_id=1, source_target_pairs={{0,1},{1,2},{2,3},{3,4},{4,5},{5,6},{6,7},{7,8},{8,9},{9,10},{10,1... | collective-permute-start | bytes 393224 | tf_op jit(solution)/shard_map/ppermute | solution.py:310
  134.5 9.4 %collective-permute-start.9 = (f32[32,1024]{1,0:T(8,128)}, f32[32,1024]{1,0:T(8,128)S(1)}, u32[]{:S(2)}, u32[]{:S(2)}) collective-permute-start(f32[32,1024]{1,0:T(8,128)} %get-tuple-element.59), channel_id=1, source_target_pairs={{1,0},{2,1},{3,2},{4,3},{5,4},{6,5},{7,6},{8,7},{9,8},{10,9},{11,1... | collective-permute-start | bytes 393224 | tf_op jit(solution)/shard_map/ppermute | solution.py:311
  136.5 4.2 %collective-permute-start.10 = (f32[4,1024]{1,0:T(4,128)}, f32[4,1024]{1,0:T(4,128)S(1)}, u32[]{:S(2)}, u32[]{:S(2)}) collective-permute-start(f32[4,1024]{1,0:T(4,128)} %get-tuple-element.60), channel_id=1, source_target_pairs={{0,16},{16,32},{32,48},{48,64},{64,80},{80,96},{96,112},{112,128},... | collective-permute-start | bytes 49160 | tf_op jit(solution)/shard_map/ppermute | solution.py:310
  139.2 4.7 %collective-permute-start.11 = (f32[4,1024]{1,0:T(4,128)}, f32[4,1024]{1,0:T(4,128)S(1)}, u32[]{:S(2)}, u32[]{:S(2)}) collective-permute-start(f32[4,1024]{1,0:T(4,128)} %get-tuple-element.61), channel_id=1, source_target_pairs={{16,0},{32,16},{48,32},{64,48},{80,64},{96,80},{112,96},{128,112},... | collective-permute-start | bytes 49160 | tf_op jit(solution)/shard_map/ppermute | solution.py:311
  140.7 3.2 %copy-start.13 = (f32[4,1024]{1,0:T(4,128)}, f32[4,1024]{1,0:T(4,128)S(1)}, u32[]{:S(2)}) copy-start(f32[4,1024]{1,0:T(4,128)S(1)} %collective-permute-done.10.refs_3_) | copy-start | bytes 49156
  143.9 0.7 copy-start.8
  148.3 15.2 %collective-permute-start.12 = (f32[32,1024]{1,0:T(8,128)}, f32[32,1024]{1,0:T(8,128)S(1)}, u32[]{:S(2)}, u32[]{:S(2)}) collective-permute-start(f32[32,1024]{1,0:T(8,128)} %get-tuple-element.64), channel_id=1, source_target_pairs={{0,1},{1,2},{2,3},{3,4},{4,5},{5,6},{6,7},{7,8},{8,9},{9,10},{10,1... | collective-permute-start | bytes 393224 | tf_op jit(solution)/shard_map/ppermute | solution.py:310
  153.4 10.1 %collective-permute-start.13 = (f32[32,1024]{1,0:T(8,128)}, f32[32,1024]{1,0:T(8,128)S(1)}, u32[]{:S(2)}, u32[]{:S(2)}) collective-permute-start(f32[32,1024]{1,0:T(8,128)} %get-tuple-element.65), channel_id=1, source_target_pairs={{1,0},{2,1},{3,2},{4,3},{5,4},{6,5},{7,6},{8,7},{9,8},{10,9},{11,1... | collective-permute-start | bytes 393224 | tf_op jit(solution)/shard_map/ppermute | solution.py:311
  155.3 4.5 %collective-permute-start.14 = (f32[4,1024]{1,0:T(4,128)}, f32[4,1024]{1,0:T(4,128)S(1)}, u32[]{:S(2)}, u32[]{:S(2)}) collective-permute-start(f32[4,1024]{1,0:T(4,128)} %get-tuple-element.66), channel_id=1, source_target_pairs={{0,16},{16,32},{32,48},{48,64},{64,80},{80,96},{96,112},{112,128},... | collective-permute-start | bytes 49160 | tf_op jit(solution)/shard_map/ppermute | solution.py:310
  158.5 5.0 %collective-permute-start.15 = (f32[4,1024]{1,0:T(4,128)}, f32[4,1024]{1,0:T(4,128)S(1)}, u32[]{:S(2)}, u32[]{:S(2)}) collective-permute-start(f32[4,1024]{1,0:T(4,128)} %get-tuple-element.67), channel_id=1, source_target_pairs={{16,0},{32,16},{48,32},{64,48},{80,64},{96,80},{112,96},{128,112},... | collective-permute-start | bytes 49160 | tf_op jit(solution)/shard_map/ppermute | solution.py:311
  159.8 3.7 %copy-start.11 = (f32[4,1024]{1,0:T(4,128)}, f32[4,1024]{1,0:T(4,128)S(1)}, u32[]{:S(2)}) copy-start(f32[4,1024]{1,0:T(4,128)S(1)} %collective-permute-done.14.refs_3_) | copy-start | bytes 49156
  (10 other events, 6.3 us)

commit v2 on v1

--- a/solution.py
+++ b/solution.py
@@ -14,11 +14,12 @@
 INTERPRET = False
 
 
-def call(body, outs, *args, specs=None):
+def call(body, outs, *args, specs=None, scratch=()):
     return pl.pallas_call(
         body,
         out_shape=outs,
         in_specs=specs or [pl.BlockSpec(memory_space=pltpu.VMEM)] * len(args),
+        scratch_shapes=scratch,
         interpret=INTERPRET,
         compiler_params=pltpu.CompilerParams(vmem_limit_bytes=60 * 2**20),
     )(*args)
@@ -151,16 +152,25 @@
     out_ref[pl.ds(1, rows, stride=2), :] = pr[:, cols:] - pi[:, :cols]
 
 
-def faces(value, xl, refs):
-    rows = value.shape[0]
-    refs[0][...] = value[:xl]
-    refs[1][...] = value[rows - xl :]
-    for layer in range(rows // xl):
-        refs[2][layer : layer + 1] = value[layer * xl : layer * xl + 1]
-        refs[3][layer : layer + 1] = value[(layer + 1) * xl - 1 : (layer + 1) * xl]
-
-
-def field_kernel(xl, data_ref, th_ref, tl_ref, log_ref, perm_ref, *face_refs):
+HALO = 4
+
+
+def edge_rows(value, xl, low_ref, high_ref, base):
+    for layer in range(value.shape[0] // xl):
+        at = base + layer * HALO
+        low_ref[at : at + HALO] = value[layer * xl : layer * xl + HALO]
+        high_ref[at : at + HALO] = value[(layer + 1) * xl - HALO : (layer + 1) * xl]
+
+
+def widen(value_ref, low_ref, high_ref, base, xl, out_ref, fill=(0.0, 0.0)):
+    for layer in range(value_ref.shape[0] // xl):
+        to, at = layer * (xl + 2 * HALO), base + layer * HALO
+        out_ref[to : to + xl] = value_ref[layer * xl : (layer + 1) * xl]
+        out_ref[to + xl : to + xl + HALO] = high_ref[at : at + HALO] + fill[1]
+        out_ref[to + xl + HALO : to + xl + 2 * HALO] = low_ref[at : at + HALO] + fill[0]
+
+
+def field_kernel(xl, data_ref, th_ref, tl_ref, log_ref, q_ref, low_ref, high_ref):
     rows, half = th_ref.shape
     mid = rows // 2
     turned = jnp.transpose(data_ref[...])
@@ -168,38 +178,16 @@
     odd = right_product(split(turned[:, mid:]), (th_ref[mid:], tl_ref[mid:]))
     log_ref[:, :half] = even + odd
     log_ref[:, half:] = even - odd
-    perm = jnp.exp(log_ref[...])
-    perm_ref[...] = perm
-    faces(perm, xl, face_refs)
-
-
-def shifted(value, halo, xl):
-    z_low, z_high, x_low, x_high = halo
-    rows, length = value.shape
-    layers = rows // xl
-    place = lax.broadcasted_iota(jnp.int32, (xl, length), 0)
-    lows, highs = [], []
-    for layer in range(layers):
-        block = value[layer * xl : (layer + 1) * xl]
-        lows.append(jnp.where(place == 0, x_low[layer : layer + 1], pltpu.roll(block, 1, 0)))
-        highs.append(jnp.where(place == xl - 1, x_high[layer : layer + 1], pltpu.roll(block, xl - 1, 0)))
-    return (
-        jnp.concatenate([z_low, value[: rows - xl]], axis=0),
-        jnp.concatenate([value[xl:], z_high], axis=0),
-        jnp.concatenate(lows, axis=0),
-        jnp.concatenate(highs, axis=0),
-        pltpu.roll(value, 1, 1),
-        pltpu.roll(value, length - 1, 1),
-    )
-
-
-def lane_sum(value, lane_at):
-    total = jnp.sum(jnp.sum(value, axis=0, keepdims=True), axis=1, keepdims=True)
-    lane = lax.broadcasted_iota(jnp.int32, (1, 128), 1)
-    return jnp.where(lane == lane_at, total, 0.0)
-
-
-def rhs_kernel(origin_ref, recharge_ref, cells_ref, rates_ref, rhs_ref, *, xl):
+    q = 0.5 * jnp.exp(-log_ref[...])
+    q_ref[...] = q
+    edge_rows(q, xl, low_ref, high_ref, 0)
+
+
+def widen_kernel(xl, edge_ref, q_ref, low_ref, high_ref, out_ref):
+    widen(q_ref, low_ref, high_ref, 0, xl, out_ref, (1.0 - edge_ref[2], 1.0 - edge_ref[3]))
+
+
+def rhs_kernel(xl, origin_ref, recharge_ref, cells_ref, rates_ref, storage_ref, rhs_ref, low_ref, high_ref):
     rows, length = recharge_ref.shape
     wells = cells_ref.shape[1]
     layer = cells_ref[0:1] - origin_ref[0]
@@ -214,46 +202,112 @@
         rate = rate - part.astype(F32)
         product = lax.dot_general(part, column, (((1,), (1,)), ((), ())), preferred_element_type=F32)
         added = product if added is None else added + product
-    rhs_ref[...] = recharge_ref[...] + added
-
-
-def setup_kernel(xl, perm_ref, h0, h1, h2, h3, storage_ref, rhs_ref, c0, c1, c2, c3, c4, c5, diag_ref, u_ref, f0, f1, f2, f3, mom_ref):
-    perm = perm_ref[...]
-    length = perm.shape[1]
-    place = lax.broadcasted_iota(jnp.int32, perm.shape, 1)
-    around = list(shifted(perm, (h0[...], h1[...], h2[...], h3[...]), xl))
-    around[4] = jnp.where(place == 0, 0.0, around[4])
-    around[5] = jnp.where(place == length - 1, 0.0, around[5])
-    twice = 2.0 * perm
-    flows = [twice * other / (perm + other) for other in around]
-    diag = storage_ref[...]
-    for flow in flows:
-        diag = diag + flow
-    inverse = 1.0 / diag
-    for ref, flow in zip((c0, c1, c2, c3, c4, c5), flows):
-        ref[...] = flow * inverse
-    rhs = rhs_ref[...]
-    u = rhs * inverse
-    diag_ref[...] = diag
-    u_ref[...] = u
-    faces(u, xl, (f0, f1, f2, f3))
-    mom_ref[...] = lane_sum(rhs * u, 0)
-
-
-def step_kernel(xl, at, last, u_ref, h0, h1, h2, h3, c0, c1, c2, c3, c4, c5, diag_ref, mom_in, new_ref, *rest):
-    around = shifted(u_ref[...], (h0[...], h1[...], h2[...], h3[...]), xl)
-    new = None
-    for coef, other in zip((c0, c1, c2, c3, c4, c5), around):
-        term = coef[...] * other
-        new = term if new is None else new + term
-    new_ref[...] = new
-    weighted = diag_ref[...] * new
-    mom = mom_in[...] + lane_sum(weighted * u_ref[...], at)
-    if last:
-        rest[0][...] = jnp.broadcast_to(mom, rest[0].shape)
-    else:
-        faces(new, xl, rest[:4])
-        rest[4][...] = mom + lane_sum(weighted * new, at + 1)
+    rhs = recharge_ref[...] + added
+    rhs_ref[...] = rhs
+    edge_rows(storage_ref[...], xl, low_ref, high_ref, 0)
+    edge_rows(rhs, xl, low_ref, high_ref, rows // xl * HALO)
+
+
+def widen_pair_kernel(xl, storage_ref, rhs_ref, low_ref, high_ref, s_ref, r_ref, first_ref, last_ref):
+    layers, wide = storage_ref.shape[0] // xl, xl + 2 * HALO
+    widen(storage_ref, low_ref, high_ref, 0, xl, s_ref)
+    widen(rhs_ref, low_ref, high_ref, layers * HALO, xl, r_ref)
+    size = (layers - 1) * wide
+    first_ref[:size] = s_ref[:size]
+    first_ref[size:] = r_ref[:size]
+    last_ref[:size] = s_ref[wide:]
+    last_ref[size:] = r_ref[wide:]
+
+
+def krylov_kernel(xl, edge_ref, q_ref, q_low, q_high, s_ref, r_ref, sr_low, sr_high, u0_out, u1_out, u2_out, u3_out, diag_out, mom_out, cz, cx, cy, inv, u0, u1, u2, u3, diag):
+    wide, length = xl + 2 * HALO, q_ref.shape[1]
+    own = q_ref.shape[0] // wide
+    total = own + 2 * HALO
+    z_lo, z_hi, x_lo, x_hi = (edge_ref[i] for i in range(4))
+    row = lax.broadcasted_iota(jnp.int32, (wide, length), 0)
+    lane = lax.broadcasted_iota(jnp.int32, (wide, length), 1)
+    keep_x = jnp.where(row == xl - 1, x_hi, jnp.where(row == wide - 1, x_lo, 1.0))
+    keep_y = jnp.where(lane == length - 1, 0.0, 1.0)
+
+    def at(z):
+        return pl.ds(z * wide, wide)
+
+    def q_of(z):
+        if z < HALO:
+            return q_low[at(z)] + (1.0 - z_lo)
+        if z >= HALO + own:
+            return q_high[at(z - HALO - own)] + (1.0 - z_hi)
+        return q_ref[at(z - HALO)]
+
+    def pair_of(z):
+        depth = own - 1
+        if z < HALO:
+            return sr_low[at(z - 1)], sr_low[at(depth + z - 1)]
+        if z >= HALO + own:
+            return sr_high[at(z - HALO - own)], sr_high[at(depth + z - HALO - own)]
+        return s_ref[at(z - HALO)], r_ref[at(z - HALO)]
+
+    def up_x(value):
+        return pltpu.roll(value, wide - 1, 0)
+
+    def down_x(value):
+        return pltpu.roll(value, 1, 0)
+
+    def up_y(value):
+        return pltpu.roll(value, length - 1, 1)
+
+    def down_y(value):
+        return pltpu.roll(value, 1, 1)
+
+    for z in range(total - 1):
+        face = pl.reciprocal(q_of(z) + q_of(z + 1))
+        if z == HALO - 1:
+            face = face * z_lo
+        if z == HALO + own - 1:
+            face = face * z_hi
+        cz[at(z)] = face
+        if z == 0:
+            continue
+        q = q_of(z)
+        storage, rhs = pair_of(z)
+        face_x = pl.reciprocal(q + up_x(q)) * keep_x
+        face_y = pl.reciprocal(q + up_y(q)) * keep_y
+        cx[at(z)] = face_x
+        cy[at(z)] = face_y
+        d = storage + cz[at(z - 1)] + face + face_x + down_x(face_x) + face_y + down_y(face_y)
+        inverse = pl.reciprocal(d)
+        inv[at(z)] = inverse
+        u0[at(z)] = rhs * inverse
+        if HALO <= z < HALO + own:
+            diag[pl.ds((z - HALO) * xl, xl)] = d[:xl]
+    levels = (u0, u1, u2, u3)
+    for level in range(3):
+        old, new = levels[level], levels[level + 1]
+        for z in range(2 + level, total - 2 - level):
+            here, face_x, face_y = old[at(z)], cx[at(z)], cy[at(z)]
+            flow = cz[at(z - 1)] * old[at(z - 1)] + cz[at(z)] * old[at(z + 1)]
+            flow = flow + face_x * up_x(here) + down_x(face_x * here)
+            flow = flow + face_y * up_y(here) + down_y(face_y * here)
+            new[at(z)] = flow * inv[at(z)]
+    sums = [None] * 6
+    for z in range(HALO, HALO + own):
+        to = pl.ds((z - HALO) * xl, xl)
+        d = diag[to]
+        values = [level[pl.ds(z * wide, xl)] for level in levels]
+        for out, value in zip((u0_out, u1_out, u2_out, u3_out), values):
+            out[to] = value
+        diag_out[to] = d
+        for i in range(6):
+            if i % 2 == 0:
+                weighted = d * values[i // 2]
+            term = weighted * values[(i + 1) // 2]
+            term = jnp.sum(term, axis=0, keepdims=True)
+            sums[i] = term if sums[i] is None else sums[i] + term
+    place = lax.broadcasted_iota(jnp.int32, (1, 128), 1)
+    moments = jnp.zeros((1, 128), F32)
+    for i in range(6):
+        moments = jnp.where(place == i, jnp.sum(sums[i], axis=1, keepdims=True), moments)
+    mom_out[...] = jnp.broadcast_to(moments, mom_out.shape)
 
 
 def partial_kernel(in_ref, out_ref):
@@ -301,45 +355,51 @@
 ITERS = 3
 
 
-def exchange(face):
-    out = []
-    for axis, low, high in (("gy", face[0], face[1]), ("gx", face[2], face[3])):
-        count = lax.axis_size(axis)
-        up = [(i, i + 1) for i in range(count - 1)]
-        down = [(i + 1, i) for i in range(count - 1)]
-        out.append(lax.ppermute(high, axis, up))
-        out.append(lax.ppermute(low, axis, down))
-    return out
+def exchange(low, high, axis):
+    count = lax.axis_size(axis)
+    up = [(i, i + 1) for i in range(count - 1)]
+    down = [(i + 1, i) for i in range(count - 1)]
+    return lax.ppermute(high, axis, up), lax.ppermute(low, axis, down)
 
 
 def shards(seeds, lengths, exponents, storage, recharge, well_cells, well_rates):
     zl, xl, length_y = storage.shape
     gx, gy = lax.axis_size("gx"), lax.axis_size("gy")
-    rows = zl * xl
-    block, zface, xface = f32(rows, length_y), f32(xl, length_y), f32(zl, length_y)
-    face_shapes = [zface, zface, xface, xface]
+    assert zl == HALO and xl >= HALO
+    rows, wide = zl * xl, xl + 2 * HALO
+    block, middle = f32(rows, length_y), f32(zl * wide, length_y)
+    edge, edge_pair = f32(zl * HALO, length_y), f32(2 * zl * HALO, length_y)
+    part = f32(2 * (zl - 1) * wide, length_y)
     at_x, at_y = lax.axis_index("gx"), lax.axis_index("gy")
     device = (at_x * gy + at_y).reshape(1).astype(jnp.int32)
     origin = jnp.stack([at_y * zl, at_x * xl]).astype(jnp.int32)
+    edges = jnp.stack([at_y > 0, at_y < gy - 1, at_x > 0, at_x < gx - 1]).astype(F32)
     smem = pl.BlockSpec(memory_space=pltpu.SMEM)
     vmem = pl.BlockSpec(memory_space=pltpu.VMEM)
     ty = halves(table_y(length_y))
     outer, twiddle, inner = tables_zx(gx, gy, zl, xl)
 
-    spectrum = call(noise_kernel, f32(length_y, rows), seeds.reshape(1, rows), *ty)
-    rhs = call(
-        lambda *refs: rhs_kernel(*refs, xl=xl),
-        block,
+    def everywhere(array):
+        return lax.all_to_all(array, ("gx", "gy"), split_axis=0, concat_axis=0, tiled=True)
+
+    flat_storage = storage.reshape(rows, length_y)
+    rhs, low, high = call(
+        lambda *refs: rhs_kernel(xl, *refs),
+        [block, edge_pair, edge_pair],
         origin,
         recharge.reshape(rows, length_y),
         well_cells,
         well_rates.reshape(1, -1),
-        specs=[smem, vmem, vmem, vmem],
-    )
-
-    def everywhere(array):
-        return lax.all_to_all(array, ("gx", "gy"), split_axis=0, concat_axis=0, tiled=True)
-
+        flat_storage,
+        specs=[smem] + [vmem] * 4,
+    )
+    low, high = exchange(low, high, "gx")
+    wide_storage, wide_rhs, first, last = call(
+        lambda *refs: widen_pair_kernel(xl, *refs), [middle, middle, part, part], flat_storage, rhs, low, high
+    )
+    pair_low, pair_high = exchange(first, last, "gy")
+
+    spectrum = call(noise_kernel, f32(length_y, rows), seeds.reshape(1, rows), *ty)
     spectrum = everywhere(spectrum)
     spectrum = call(
         lambda *refs: spectrum_kernel((gx, gy, zl, xl, length_y), *refs),
@@ -357,33 +417,28 @@
         specs=[smem, smem, smem] + [vmem] * 11,
     )
     spectrum = everywhere(spectrum)
-    log_perm, perm, *face = call(
-        lambda *refs: field_kernel(xl, *refs), [block, block] + face_shapes, spectrum, *ty
-    )
-    *coefs, diag, u0, f0, f1, f2, f3, moments = call(
-        lambda *refs: setup_kernel(xl, *refs),
-        [block] * 8 + face_shapes + [f32(1, 128)],
-        perm,
-        *exchange(face),
-        storage.reshape(rows, length_y),
-        rhs,
-    )
-    face = (f0, f1, f2, f3)
-    basis = [u0]
-    for step in range(ITERS):
-        last = step + 1 == ITERS
-        outs = [block, f32(gx, 128)] if last else [block] + face_shapes + [f32(1, 128)]
-        new, *rest = call(
-            lambda *refs, step=step, last=last: step_kernel(xl, 2 * step + 1, last, *refs),
-            outs,
-            basis[-1],
-            *exchange(face),
-            *coefs,
-            diag,
-            moments,
-        )
-        basis.append(new)
-        face, moments = rest[:4], rest[-1]
+    log_perm, q, low, high = call(
+        lambda *refs: field_kernel(xl, *refs), [block, block, edge, edge], spectrum, *ty
+    )
+    low, high = exchange(low, high, "gx")
+    q = call(lambda *refs: widen_kernel(xl, *refs), middle, edges, q, low, high, specs=[smem] + [vmem] * 3)
+    q_low, q_high = exchange(q, q, "gy")
+
+    layers = zl + 2 * HALO
+    *basis, diag, moments = call(
+        lambda *refs: krylov_kernel(xl, *refs),
+        [block] * 5 + [f32(gx, 128)],
+        edges,
+        q,
+        q_low,
+        q_high,
+        wide_storage,
+        wide_rhs,
+        pair_low,
+        pair_high,
+        specs=[smem] + [vmem] * 7,
+        scratch=[pltpu.VMEM((layers * wide, length_y), F32)] * 8 + [pltpu.VMEM((rows, length_y), F32)],
+    )
     moments = lax.all_to_all(moments, "gx", split_axis=0, concat_axis=0, tiled=True)
     moments = call(partial_kernel, f32(gy, 128), moments)
     moments = lax.all_to_all(moments, "gy", split_axis=0, concat_axis=0, tiled=True)

time: 211 us -> 172 us (0.82)
  blocking collectives: 70.7 us -> 36.8 us
  starting transfers between devices: 65.3 us -> 54.6 us
  waiting for transfers between devices: 32.5 us -> 40.7 us
  Pallas kernels: 35 us -> 31.6 us
    all_to_all x1 -> x0, blocking collectives: 33.1 us -> none  [everywhere(): lax.all_to_all(array, ('gx', 'gy'), split_axis=0, concat_axis=0, tiled=True)]
    ppermute x16 -> x8, starting transfers between devices: 43.2 us -> 23.3 us  [exchange(): return (lax.ppermute(high, axis, up), lax.ppermute(low, axis, down))]
    all_to_all x1 -> x2, starting transfers between devices: 22.2 us -> 31.3 us  [everywhere(): lax.all_to_all(array, ('gx', 'gy'), split_axis=0, concat_axis=0, tiled=True)]
    ppermute x16 -> x8, waiting for transfers between devices: 10.5 us -> 18.8 us  [exchange(): return (lax.ppermute(high, axis, up), lax.ppermute(low, axis, down))]
    pallas_call x10 -> x9, Pallas kernels: 35 us -> 31.6 us  [call(): pl.pallas_call(body, out_shape=outs, in_specs=specs or [pl.BlockSpec(memo...]
    all_to_all x1 -> x2, waiting for transfers between devices: 21.9 us -> 21.9 us  [everywhere(): lax.all_to_all(array, ('gx', 'gy'), split_axis=0, concat_axis=0, tiled=True)]
  transfers between devices with their start and end apart: 17 -> 10, of which waited for: 5 -> 6; matrix products, arithmetic and copies ran while one was open for 0% -> 1% of each run, Pallas kernels for 1% -> 7%
where the time goes in v2:
time: 172 us; the launch traced here: 171 us
  starting transfers between devices  54.6 us (32%)
  waiting for transfers between devices  40.7 us (24%)
  blocking collectives  36.8 us (21%)
  Pallas kernels  31.6 us (18%)
  local copies, waits for them, and re-layouts  4.98 us (3%)
    pallas_call x9, Pallas kernels, call(): pl.pallas_call(body, out_shape=outs, in_specs=specs or [pl.BlockSpec(memo...  31.6 us
    all_to_all x2, starting transfers between devices, everywhere(): lax.all_to_all(array, ('gx', 'gy'), split_axis=0, concat_axis=0, tiled=True)  31.3 us
    ppermute x8, starting transfers between devices, exchange(): return (lax.ppermute(high, axis, up), lax.ppermute(low, axis, down))  23.3 us
    all_to_all x2, waiting for transfers between devices, everywhere(): lax.all_to_all(array, ('gx', 'gy'), split_axis=0, concat_axis=0, tiled=True)  21.9 us
    all_to_all x1, blocking collectives, shards(): lax.all_to_all(moments, 'gx', split_axis=0, concat_axis=0, tiled=True)  18.8 us
    ppermute x8, waiting for transfers between devices, exchange(): return (lax.ppermute(high, axis, up), lax.ppermute(low, axis, down))  18.8 us
    all_to_all x1, blocking collectives, shards(): lax.all_to_all(moments, 'gy', split_axis=0, concat_axis=0, tiled=True)  18 us
    unnamed x20, local copies, waits for them, and re-layouts  3.7 us
  transfers between devices with their start and end apart: 10, of which 6 were waited for; matrix products, arithmetic and copies ran while one was open for 1% of the time, Pallas kernels for 7%

profile of v2, /device:TPU:1, one launch (start us, length us, event | category | flops | bytes accessed | tf_op | source)
XLA Modules:
  0.0 170.8 jit_solution(13558732572143606915)
XLA Ops:
  1.9 3.5 %shard_map.202 = f32[1024,128]{1,0:T(8,128)} custom-call(s32[1,128]{1,0:T(1,128)} %reshape.39.seed_ref, bf16[1024,512]{1,0:T(8,128)(2,1)} %constant.45.clone.th_ref.refs_1_, bf16[1024,512]{1,0:T(8,128)(2,1)} %constant.46.clone.tl_ref.refs_2_), custom_call_target="tpu_custom_call" | custom-call | tf_op jit(solution)/shard_map/pallas_call | solution.py:18
  5.4 22.2 %all-to-all-start = ((f32[512,2,128]{2,1,0:T(2,128)}), f32[512,2,128]{2,1,0:T(2,128)S(1)}, u32[]{:S(2)}, u32[]{:S(2)}) async-start(f32[512,2,128]{2,1,0:T(2,128)} %bitcast.30), calls=%async_computation | async-start | bytes 1048576 | tf_op jit(solution)/shard_map/all_to_all | solution.py:383
  27.6 21.9 %all-to-all-done = f32[512,2,128]{2,1,0:T(2,128)S(1)} async-done(((f32[512,2,128]{2,1,0:T(2,128)}), f32[512,2,128]{2,1,0:T(2,128)S(1)}, u32[]{:S(2)}, u32[]{:S(2)}) %all-to-all-start) | async-done | bytes 524320 | tf_op jit(solution)/shard_map/all_to_all | solution.py:383
  50.3 5.5 %shard_map.203 = f32[1024,128]{1,0:T(8,128)} custom-call(s32[1]{0:T(128)} %bitcast.refs_0_, f32[3]{0:T(128)} %refs_1_.2, f32[3]{0:T(128)} %refs_2_.3, f32[1024,128]{1,0:T(8,128)} %bitcast.27, bf16[512,512]{1,0:T(8,128)(2,1)} %constant.47.clone.refs_4_, bf16[512,512]{1,0:T(8,128)(2,1)} %constant.48.clone.refs_5_, bf16[512,512]{1,0:T(8,128)(2,1)} %constant.49.clone.refs_6_, ...), custom_call_target="tpu_custom_call" | custom-call | tf_op jit(solution)/shard_map/pallas_call | solution.py:18
  55.8 9.1 %all-to-all-start.1 = ((f32[512,2,128]{2,1,0:T(2,128)}), f32[512,2,128]{2,1,0:T(2,128)S(1)}, u32[]{:S(2)}, u32[]{:S(2)}) async-start(f32[512,2,128]{2,1,0:T(2,128)} %bitcast.25), calls=%async_computation.1 | async-start | bytes 1048576 | tf_op jit(solution)/shard_map/all_to_all | solution.py:383
  65.6 2.7 %shard_map.206 = (f32[128,1024]{1,0:T(8,128)}, f32[32,1024]{1,0:T(8,128)}, f32[32,1024]{1,0:T(8,128)}) custom-call(s32[2]{0:T(128)} %pad_add_fusion.refs_0_, f32[128,1024]{1,0:T(8,128)} %bitcast.31, s32[3,256]{1,0:T(4,128)} %refs_2_.4, f32[1,256]{1,0:T(1,128)} %bitcast.36, f32[128,1024]{1,0:T(8,128)} %bitcast.28), custom_call_target="tpu_custom_call" | custom-call | tf_op jit(solution)/shard_map/pallas_call | solution.py:18
  68.4 3.8 %collective-permute-start.4 = (f32[32,1024]{1,0:T(8,128)}, f32[32,1024]{1,0:T(8,128)S(1)}, u32[]{:S(2)}, u32[]{:S(2)}) collective-permute-start(f32[32,1024]{1,0:T(8,128)} %get-tuple-element.27), channel_id=1, source_target_pairs={{0,16},{16,32},{32,48},{48,64},{64,80},{80,96},{96,112},{112,128},... | collective-permute-start | bytes 393224 | tf_op jit(solution)/shard_map/ppermute | solution.py:362
  73.5 5.6 %collective-permute-done.4.refs_2_ = f32[32,1024]{1,0:T(8,128)S(1)} collective-permute-done((f32[32,1024]{1,0:T(8,128)}, f32[32,1024]{1,0:T(8,128)S(1)}, u32[]{:S(2)}, u32[]{:S(2)}) %collective-permute-start.4) | collective-permute-done | bytes 131104 | tf_op jit(solution)/shard_map/ppermute | solution.py:362
  79.0 1.5 collective-permute-done.5.refs_3_
  81.2 3.0 %shard_map.207 = (f32[160,1024]{1,0:T(8,128)}, f32[160,1024]{1,0:T(8,128)}, f32[240,1024]{1,0:T(8,128)}, f32[240,1024]{1,0:T(8,128)}) custom-call(f32[128,1024]{1,0:T(8,128)} %bitcast.29, f32[128,1024]{1,0:T(8,128)} %get-tuple-element.26.refs_1_, f32[32,1024]{1,0:T(8,128)} %copy-done.6, f32[32,1024]{1,0:T(8,128)} %copy-done.7), custom_call_target="tpu_custom_call" | custom-call | tf_op jit(solution)/shard_map/pallas_call | solution.py:18
  84.2 4.2 %collective-permute-start.6 = (f32[240,1024]{1,0:T(8,128)}, f32[240,1024]{1,0:T(8,128)S(1)}, u32[]{:S(2)}, u32[]{:S(2)}) collective-permute-start(f32[240,1024]{1,0:T(8,128)} %get-tuple-element.31), channel_id=1, source_target_pairs={{0,1},{1,2},{2,3},{3,4},{4,5},{5,6},{6,7},{7,8},{8,9},{9,10},{10,1... | collective-permute-start | bytes 2949128 | tf_op jit(solution)/shard_map/ppermute | solution.py:362
  88.5 1.9 %collective-permute-start.7 = (f32[240,1024]{1,0:T(8,128)}, f32[240,1024]{1,0:T(8,128)S(1)}, u32[]{:S(2)}, u32[]{:S(2)}) collective-permute-start(f32[240,1024]{1,0:T(8,128)} %get-tuple-element.32), channel_id=1, source_target_pairs={{1,0},{2,1},{3,2},{4,3},{5,4},{6,5},{7,6},{8,7},{9,8},{10,9},{11,1... | collective-permute-start | bytes 2949128 | tf_op jit(solution)/shard_map/ppermute | solution.py:362
  91.2 3.4 %shard_map.204 = (f32[128,1024]{1,0:T(8,128)}, f32[128,1024]{1,0:T(8,128)}, f32[16,1024]{1,0:T(8,128)}, f32[16,1024]{1,0:T(8,128)}) custom-call(f32[1024,128]{1,0:T(8,128)} %bitcast.26, bf16[1024,512]{1,0:T(8,128)(2,1)} %constant.45.clone.th_ref.refs_1_, bf16[1024,512]{1,0:T(8,128)(2,1)} %constant.46.clone.tl_ref.refs_2_), custom_call_target="tpu_custom_call" | custom-call | tf_op jit(solution)/shard_map/pallas_call | solution.py:18
  94.6 3.9 %collective-permute-start = (f32[16,1024]{1,0:T(8,128)}, f32[16,1024]{1,0:T(8,128)S(1)}, u32[]{:S(2)}, u32[]{:S(2)}) collective-permute-start(f32[16,1024]{1,0:T(8,128)} %get-tuple-element.24), channel_id=1, source_target_pairs={{0,16},{16,32},{32,48},{48,64},{64,80},{80,96},{96,112},{112,128},... | collective-permute-start | bytes 196616 | tf_op jit(solution)/shard_map/ppermute | solution.py:362
  100.4 4.1 %collective-permute-done.1.refs_3_ = f32[16,1024]{1,0:T(8,128)S(1)} collective-permute-done((f32[16,1024]{1,0:T(8,128)}, f32[16,1024]{1,0:T(8,128)S(1)}, u32[]{:S(2)}, u32[]{:S(2)}) %collective-permute-start.1) | collective-permute-done | bytes 65568 | tf_op jit(solution)/shard_map/ppermute | solution.py:362
  105.1 2.0 %shard_map.205.refs_1_ = f32[160,1024]{1,0:T(8,128)} custom-call(f32[4]{0:T(128)} %add_convert_fusion.refs_0_, f32[128,1024]{1,0:T(8,128)} %get-tuple-element.23.refs_1_, f32[16,1024]{1,0:T(8,128)} %copy-done.8, f32[16,1024]{1,0:T(8,128)} %copy-done.9), custom_call_target="tpu_custom_call" | custom-call | tf_op jit(solution)/shard_map/pallas_call | solution.py:18
  107.1 1.9 %collective-permute-start.3 = (f32[160,1024]{1,0:T(8,128)}, f32[160,1024]{1,0:T(8,128)S(1)}, u32[]{:S(2)}, u32[]{:S(2)}) collective-permute-start(f32[160,1024]{1,0:T(8,128)} %shard_map.205.refs_1_), channel_id=1, source_target_pairs={{1,0},{2,1},{3,2},{4,3},{5,4},{6,5},{7,6},{8,7},{9,8},{10,9},{11,1... | collective-permute-start | bytes 1966088 | tf_op jit(solution)/shard_map/ppermute | solution.py:362
  109.0 5.0 %collective-permute-start.2 = (f32[160,1024]{1,0:T(8,128)}, f32[160,1024]{1,0:T(8,128)S(1)}, u32[]{:S(2)}, u32[]{:S(2)}) collective-permute-start(f32[160,1024]{1,0:T(8,128)} %shard_map.205.refs_1_), channel_id=1, source_target_pairs={{0,1},{1,2},{2,3},{3,4},{4,5},{5,6},{6,7},{7,8},{8,9},{9,10},{10,1... | collective-permute-start | bytes 1966088 | tf_op jit(solution)/shard_map/ppermute | solution.py:362
  114.1 6.3 %collective-permute-done.3.refs_3_ = f32[160,1024]{1,0:T(8,128)S(1)} collective-permute-done((f32[160,1024]{1,0:T(8,128)}, f32[160,1024]{1,0:T(8,128)S(1)}, u32[]{:S(2)}, u32[]{:S(2)}) %collective-permute-start.3) | collective-permute-done | bytes 655392 | tf_op jit(solution)/shard_map/ppermute | solution.py:362
  122.5 7.0 %shard_map.208 = (f32[128,1024]{1,0:T(8,128)}, f32[128,1024]{1,0:T(8,128)}, f32[128,1024]{1,0:T(8,128)}, f32[128,1024]{1,0:T(8,128)}, f32[128,1024]{1,0:T(8,128)}, /*index=5*/f32[32,128]{1,0:T(8,128)}) custom-call(f32[4]{0:T(128)} %add_convert_fusion.refs_0_, f32[160,1024]{1,0:T(8,128)} %shard_map.205.refs_1_, f32[160,1024]{1,0:T(8,128)} %copy-done.5, ...), custom_call_target="tpu_custom_call" | custom-call | tf_op jit(solution)/shard_map/pallas_call | solution.py:18
  129.5 18.8 %all_to_all.44 = f32[32,1,128]{2,1,0:T(1,128)} all-to-all(f32[32,1,128]{2,1,0:T(1,128)} %bitcast.35), channel_id=1, replica_groups=mesh['gx'=32,'gy'=16] {'gx'}, dimensions={0} | all-to-all | bytes 32768 | tf_op jit(solution)/shard_map/all_to_all | solution.py:442
  148.3 1.3 shard_map.209
  149.6 18.0 %all_to_all.45 = f32[16,1,128]{2,1,0:T(1,128)} all-to-all(f32[16,1,128]{2,1,0:T(1,128)} %bitcast.34), channel_id=1, replica_groups=mesh['gx'=32,'gy'=16] {'gy'}, dimensions={0} | all-to-all | bytes 16384 | tf_op jit(solution)/shard_map/all_to_all | solution.py:444
  167.6 3.1 %shard_map.210 = (f32[128,1024]{1,0:T(8,128)}, f32[128,1024]{1,0:T(8,128)}) custom-call(f32[16,128]{1,0:T(8,128)} %bitcast.33, f32[128,1024]{1,0:T(8,128)} %get-tuple-element.34.refs_1_, f32[128,1024]{1,0:T(8,128)} %get-tuple-element.35.refs_2_, f32[128,1024]{1,0:T(8,128)} %get-tuple-element.36.refs_3_, f32[128,1024]{1,0:T(8,128)} %get-tuple-element.37.refs_4_, ...), custom_call_target="tpu_custom_call" | custom-call | tf_op jit(solution)/shard_map/pallas_call | solution.py:18
  (30 shorter events, 10.1 us)
Async XLA Ops:
  5.4 44.1 %all-to-all-start = ((f32[512,2,128]{2,1,0:T(2,128)}), f32[512,2,128]{2,1,0:T(2,128)S(1)}, u32[]{:S(2)}, u32[]{:S(2)}) async-start(f32[512,2,128]{2,1,0:T(2,128)} %bitcast.30), calls=%async_computation | async-start | bytes 1048576 | tf_op jit(solution)/shard_map/all_to_all | solution.py:383
  49.5 0.8 copy-start.1
  55.8 34.6 %all-to-all-start.1 = ((f32[512,2,128]{2,1,0:T(2,128)}), f32[512,2,128]{2,1,0:T(2,128)S(1)}, u32[]{:S(2)}, u32[]{:S(2)}) async-start(f32[512,2,128]{2,1,0:T(2,128)} %bitcast.25), calls=%async_computation.1 | async-start | bytes 1048576 | tf_op jit(solution)/shard_map/all_to_all | solution.py:383
  68.4 10.7 %collective-permute-start.4 = (f32[32,1024]{1,0:T(8,128)}, f32[32,1024]{1,0:T(8,128)S(1)}, u32[]{:S(2)}, u32[]{:S(2)}) collective-permute-start(f32[32,1024]{1,0:T(8,128)} %get-tuple-element.27), channel_id=1, source_target_pairs={{0,16},{16,32},{32,48},{48,64},{64,80},{80,96},{96,112},{112,128},... | collective-permute-start | bytes 393224 | tf_op jit(solution)/shard_map/ppermute | solution.py:362
  72.2 8.4 %collective-permute-start.5 = (f32[32,1024]{1,0:T(8,128)}, f32[32,1024]{1,0:T(8,128)S(1)}, u32[]{:S(2)}, u32[]{:S(2)}) collective-permute-start(f32[32,1024]{1,0:T(8,128)} %get-tuple-element.28), channel_id=1, source_target_pairs={{16,0},{32,16},{48,32},{64,48},{80,64},{96,80},{112,96},{128,112},... | collective-permute-start | bytes 393224 | tf_op jit(solution)/shard_map/ppermute | solution.py:362
  79.0 1.5 copy-start.6
  80.5 0.7 copy-start.7
  84.2 29.8 %collective-permute-start.6 = (f32[240,1024]{1,0:T(8,128)}, f32[240,1024]{1,0:T(8,128)S(1)}, u32[]{:S(2)}, u32[]{:S(2)}) collective-permute-start(f32[240,1024]{1,0:T(8,128)} %get-tuple-element.31), channel_id=1, source_target_pairs={{0,1},{1,2},{2,3},{3,4},{4,5},{5,6},{6,7},{7,8},{8,9},{9,10},{10,1... | collective-permute-start | bytes 2949128 | tf_op jit(solution)/shard_map/ppermute | solution.py:362
  88.5 25.6 %collective-permute-start.7 = (f32[240,1024]{1,0:T(8,128)}, f32[240,1024]{1,0:T(8,128)S(1)}, u32[]{:S(2)}, u32[]{:S(2)}) collective-permute-start(f32[240,1024]{1,0:T(8,128)} %get-tuple-element.32), channel_id=1, source_target_pairs={{1,0},{2,1},{3,2},{4,3},{5,4},{6,5},{7,6},{8,7},{9,8},{10,9},{11,1... | collective-permute-start | bytes 2949128 | tf_op jit(solution)/shard_map/ppermute | solution.py:362
  90.4 0.8 copy-start
  94.6 5.8 %collective-permute-start = (f32[16,1024]{1,0:T(8,128)}, f32[16,1024]{1,0:T(8,128)S(1)}, u32[]{:S(2)}, u32[]{:S(2)}) collective-permute-start(f32[16,1024]{1,0:T(8,128)} %get-tuple-element.24), channel_id=1, source_target_pairs={{0,16},{16,32},{32,48},{48,64},{64,80},{80,96},{96,112},{112,128},... | collective-permute-start | bytes 196616 | tf_op jit(solution)/shard_map/ppermute | solution.py:362
  98.5 6.0 %collective-permute-start.1 = (f32[16,1024]{1,0:T(8,128)}, f32[16,1024]{1,0:T(8,128)S(1)}, u32[]{:S(2)}, u32[]{:S(2)}) collective-permute-start(f32[16,1024]{1,0:T(8,128)} %get-tuple-element.25), channel_id=1, source_target_pairs={{16,0},{32,16},{48,32},{64,48},{80,64},{96,80},{112,96},{128,112},... | collective-permute-start | bytes 196616 | tf_op jit(solution)/shard_map/ppermute | solution.py:362
  100.4 4.1 %copy-start.8 = (f32[16,1024]{1,0:T(8,128)}, f32[16,1024]{1,0:T(8,128)S(1)}, u32[]{:S(2)}) copy-start(f32[16,1024]{1,0:T(8,128)S(1)} %collective-permute-done.refs_2_) | copy-start | bytes 196612
  104.5 0.6 copy-start.9
  107.1 13.3 %collective-permute-start.3 = (f32[160,1024]{1,0:T(8,128)}, f32[160,1024]{1,0:T(8,128)S(1)}, u32[]{:S(2)}, u32[]{:S(2)}) collective-permute-start(f32[160,1024]{1,0:T(8,128)} %shard_map.205.refs_1_), channel_id=1, source_target_pairs={{1,0},{2,1},{3,2},{4,3},{5,4},{6,5},{7,6},{8,7},{9,8},{10,9},{11,1... | collective-permute-start | bytes 1966088 | tf_op jit(solution)/shard_map/ppermute | solution.py:362
  109.0 12.6 %collective-permute-start.2 = (f32[160,1024]{1,0:T(8,128)}, f32[160,1024]{1,0:T(8,128)S(1)}, u32[]{:S(2)}, u32[]{:S(2)}) collective-permute-start(f32[160,1024]{1,0:T(8,128)} %shard_map.205.refs_1_), channel_id=1, source_target_pairs={{0,1},{1,2},{2,3},{3,4},{4,5},{5,6},{6,7},{7,8},{8,9},{9,10},{10,1... | collective-permute-start | bytes 1966088 | tf_op jit(solution)/shard_map/ppermute | solution.py:362
  114.0 7.6 %copy-start.2 = (f32[240,1024]{1,0:T(8,128)}, f32[240,1024]{1,0:T(8,128)S(1)}, u32[]{:S(2)}) copy-start(f32[240,1024]{1,0:T(8,128)S(1)} %collective-permute-done.6.refs_6_) | copy-start | bytes 2949124
  114.1 7.6 %copy-start.3 = (f32[240,1024]{1,0:T(8,128)}, f32[240,1024]{1,0:T(8,128)S(1)}, u32[]{:S(2)}) copy-start(f32[240,1024]{1,0:T(8,128)S(1)} %collective-permute-done.7.refs_7_) | copy-start | bytes 2949124
  120.4 1.3 copy-start.4
  121.7 0.8 copy-start.5
